TPU v7x, 256 devices: a whole 4x4x8 slice. The times are simulated.
256 devices in a mesh: slab: 32 (over x, z), grp: 8 (over y, core).
Axes of the slice: x: 4, y: 4, z: 8, core: 2. Of those that a mesh axis runs over, the one named last changes fastest.
Arguments:
- tile_centres: int32 [3, 8192], P(None, ('slab', 'grp')), may hold values from 0 to 511, as said below
- tile_coeffs: float32 [64, 8192], P(None, ('slab', 'grp')), may hold values from -4 to 4
- tile_exponents: float32 [8192], P(('slab', 'grp')), may hold values from 0.02 to 0.3
- tile_live: int32 [8192], P(('slab', 'grp')), may hold values from 0 to 1, as said below
Outputs:
- spectrum: float32 [2, 256, 512, 256], P(None, 'slab', 'grp')
Inputs may be any that keep to these rules, and one draw needn't show every extreme that they name: `tile_centres`: row 0 holds a tile's cell along the first dimension (below 512), row 1 along the second (below 512), row 2 along the third; the third coordinate of tile p lies in [(p // 256) * 8, (p // 256 + 1) * 8). `tile_live`: 1 for a slot that holds a tile, 0 for an empty one.
All inputs are finite; a program needn't handle non-finite values.
Results may differ from a plain program's by a relative error of at most 0.0001.
Values sent between devices are 32-bit elements; how exact they have to be, the bound alone decides.
No kernel may reach another device: no remote copies, remote signals or barrier semaphores. Data moves between devices by JAX's collectives and lax.ppermute only.
A program may use at most 128 MiB of HBM per device.

v0:
```python
import functools
import math

import jax
import jax.numpy as jnp
import numpy as np
from jax import lax
from jax.experimental import pallas as pl
from jax.experimental.pallas import tpu as pltpu
from jax.sharding import PartitionSpec as P

NX = 512
NY = 512
CZ = 8
HALF = 8
NPOW = 4
TERMS = NPOW * NPOW * NPOW
LANES = 128
ROWS = 17
FEAT = 72
SLOTS = 96
BLOCK = 56
COUNT_X = 4
NT = (((1,), (1,)), ((), ()))
F32 = jnp.float32
BF16 = jnp.bfloat16


def split(value):
    high = value.astype(BF16)
    return high, (value - high.astype(F32)).astype(BF16)


def pack_kernel(copies, coeffs_ref, centres_ref, exponents_ref, live_ref, out_ref, block):
    half = coeffs_ref.shape[0] // 2
    block[0:half, 0:TERMS] = coeffs_ref[0:half, :]
    block[0:half, TERMS:] = coeffs_ref[half:, :]
    centres = centres_ref[...].astype(F32)
    alive = live_ref[...] > 0
    width = 2 * half
    block[half : half + 1, 0:width] = exponents_ref[...]
    block[half : half + 1, width : 2 * width] = centres[0:1]
    block[half : half + 1, 2 * width : 3 * width] = jnp.where(alive, centres[1:2], -1.0)
    block[half : half + 1, 3 * width : 4 * width] = centres[2:3]
    value = block[...]
    for copy in range(copies):
        out_ref[copy * ROWS : (copy + 1) * ROWS, :] = value


def pack_tiles(copies, tile_centres, tile_coeffs, tile_exponents, tile_live):
    return pl.pallas_call(
        functools.partial(pack_kernel, copies),
        out_shape=jax.ShapeDtypeStruct((copies * ROWS, LANES), F32),
        scratch_shapes=[pltpu.VMEM((ROWS, LANES), F32)],
        name="pack_tiles",
    )(tile_coeffs.T, tile_centres, tile_exponents[None, :], tile_live[None, :])


def route_kernel(sources, groups, tri_ref, scalar_ref, tiles_ref, out_ref, rows_ref, table, rank_ref, count_ref):
    per_row = 16
    side = sources * per_row
    total = 2 * side
    for source in range(sources):
        rows_ref[source * per_row : (source + 1) * per_row, :] = tiles_ref[
            source * ROWS : source * ROWS + per_row, :
        ]
    turned = rows_ref[...].T
    table[0:TERMS, 0:side] = turned[0:TERMS]
    table[0:TERMS, side:total] = turned[TERMS:]
    misc = tiles_ref[pl.ds(per_row, sources, stride=ROWS), :]
    sublane = lax.broadcasted_iota(jnp.int32, (8, LANES), 0)
    lane = lax.broadcasted_iota(jnp.int32, (8, LANES), 1)
    own = lane // per_row == sublane
    table[TERMS:, :] = jnp.zeros((table.shape[0] - TERMS, total), F32)
    for part in range(sources // 8):
        piece = misc[part * 8 : (part + 1) * 8]
        fanned = pltpu.roll(piece, 0, 1, stride=per_row, stride_axis=0)
        for kind in range(4):
            for which in range(2):
                start = kind * 2 * per_row + which * per_row
                moved = pltpu.roll(fanned, LANES - start, 1) if start else fanned
                row = jnp.sum(jnp.where(own, moved, 0.0), axis=0, keepdims=True)
                at = which * side + part * LANES
                table[TERMS + kind : TERMS + kind + 1, at : at + LANES] = row
    centre_y = table[TERMS + 2 : TERMS + 3, :].astype(jnp.int32)
    rows_own = NY // groups
    group = lax.broadcasted_iota(jnp.int32, (groups, 1), 0)
    reach = (centre_y - group * rows_own + HALF) & (NY - 1)
    reach = jnp.where(centre_y >= 0, reach, NY)
    edges = (0, rows_own // 2, rows_own // 2 + 2 * HALF, rows_own + 2 * HALF)
    tri = tri_ref[...]
    step = tri.shape[0]
    marks = []
    for kind in range(3):
        inside = jnp.where((reach >= edges[kind]) & (reach < edges[kind + 1]), 1.0, 0.0)
        for part in range(total // step):
            marks.append(inside[:, part * step : (part + 1) * step])
    before = jnp.dot(jnp.concatenate(marks, axis=0).astype(BF16), tri, preferred_element_type=F32)
    rank_ref[...] = jnp.full(rank_ref.shape, -1.0, F32)
    count = jnp.zeros((groups, 1), F32)
    index = 0
    for kind in range(3):
        for part in range(total // step):
            lanes = slice(part * step, (part + 1) * step)
            found = before[index * groups : (index + 1) * groups] + count
            rank_ref[:, lanes] = jnp.where(marks[index] > 0.0, found, rank_ref[:, lanes])
            count = count + jnp.sum(marks[index], axis=1, keepdims=True)
            index += 1
        count_ref[kind] = jnp.broadcast_to(count, (groups, LANES))
    base = (scalar_ref[0] * SLOTS).astype(F32)
    core = scalar_ref[1]
    high, low = split(table[...])
    both = jnp.concatenate([high, low], axis=0)
    depth = table.shape[0]
    most = jnp.max(count)
    slot = lax.broadcasted_iota(jnp.int32, (LANES, total), 0).astype(F32)
    lane = lax.broadcasted_iota(jnp.int32, (32, LANES), 1)
    rows_y = groups // 2
    for target in range(rows_y):
        own_row = pl.ds(2 * target + core, 1)
        ranks = rank_ref[own_row, :] - base
        pick = jnp.where(slot == ranks, 1.0, 0.0).astype(BF16)
        got = lax.dot_general(both, pick, NT, preferred_element_type=F32)
        got = got[0:FEAT] + got[depth : depth + FEAT]
        first = jnp.where(lane < 64, got[0:32], pltpu.roll(got[32:64], 64, 1))
        rest = [got[16 * q : 16 * q + 16] for q in range(4)]
        quarter = lane[0:16] // 32
        extra = pltpu.roll(rest[0], 64, 1)
        extra = jnp.where(quarter == 1, pltpu.roll(rest[1], 96, 1), extra)
        extra = jnp.where(quarter == 2, rest[2], extra)
        extra = jnp.where(quarter == 3, pltpu.roll(rest[3], 32, 1), extra)
        ends = [jnp.clip(count_ref[kind, own_row, :] - base, 0.0, float(SLOTS)) for kind in range(3)]
        numbers = jnp.concatenate(
            [got[TERMS : TERMS + 4], ends[2], ends[1], ends[0], jnp.full((1, LANES), most, F32)], axis=0
        )
        for copy in range(out_ref.shape[0] // (BLOCK * rows_y)):
            at = (copy * rows_y + target) * BLOCK
            out_ref[at : at + 32, :] = first
            out_ref[at + 32 : at + 48, :] = extra
            out_ref[at + 48 : at + 56, :] = numbers


def route_tiles(sources, targets, groups, tri, scalars, tiles):
    return pl.pallas_call(
        functools.partial(route_kernel, sources, groups),
        in_specs=[
            pl.BlockSpec(memory_space=pltpu.VMEM),
            pl.BlockSpec(memory_space=pltpu.SMEM),
            pl.BlockSpec(memory_space=pltpu.VMEM),
        ],
        out_specs=pl.BlockSpec(memory_space=pltpu.VMEM),
        out_shape=jax.ShapeDtypeStruct((targets * BLOCK, LANES), F32),
        scratch_shapes=[
            pltpu.VMEM((sources * 16, LANES), F32),
            pltpu.VMEM((80, sources * 32), F32),
            pltpu.VMEM((groups, sources * 32), F32),
            pltpu.VMEM((3, groups, LANES), F32),
        ],
        name="route_tiles",
    )(tri, scalars, tiles)


def powers_of(distance, rate):
    square = distance * distance
    envelope = jnp.where(square <= float(HALF * HALF), jnp.exp(square * rate), 0.0)
    scaled = distance * (1.0 / HALF)
    found = [envelope]
    for _ in range(NPOW - 1):
        found.append(found[-1] * scaled)
    return found


def merge_sources(sources, tiles_ref, bins):
    lane = lax.broadcasted_iota(jnp.int32, (8, LANES), 1)
    ends = [jnp.int32(0), jnp.int32(0)]
    for source in range(sources):
        block = tiles_ref.at[source]
        held, upto, start = (
            jnp.max(block[52 + k : 53 + k, :]).astype(jnp.int32) for k in range(3)
        )
        pieces = []
        for row in range(0, 32, 8):
            extra = block[32 + row % 16 : 40 + row % 16, :]
            pieces.append(
                jnp.where(lane < 64, block[row : row + 8, :], pltpu.roll(extra, 64 if row < 16 else 32, 1))
            )
        for row in range(0, 32, 8):
            extra = block[32 + row % 16 : 40 + row % 16, :]
            extra = extra if row < 16 else pltpu.roll(extra, 96, 1)
            pieces.append(jnp.where(lane < 64, pltpu.roll(block[row : row + 8, :], 64, 1), extra))
        pieces.append(block[48:56, :])
        for half, (begin, end) in enumerate(((jnp.int32(0), upto), (start, held))):
            valid = (lane >= begin) & (lane < end)
            column = ends[half] // LANES
            offset = ends[half] % LANES
            shift = (offset - begin + LANES) % LANES
            for part, piece in enumerate(pieces):
                moved = pltpu.roll(jnp.where(valid, piece, 0.0), shift, 1)
                rows = slice(8 * part, 8 * part + 8)
                bins[half, column, rows, :] = jnp.where(lane < offset, bins[half, column, rows, :], moved)
                bins[half, column + 1, rows, :] = jnp.where(lane < offset, moved, 0.0)
            ends[half] = ends[half] + (end - begin)
    return ends


def spectrum_kernel(
    sources, groups, kx_own, depth, place_ref, tiles_ref, wave_high_ref, wave_low_ref,
    out_ref, most_ref, bins, total, lhs_0, lhs_1, rhs_0, rhs_1, weights_0, weights_1, turn_ref, stage, sems,
):
    rows_own = NY // groups
    rows_half = rows_own // 2
    first_kx = place_ref[0] * kx_own
    first_y = place_ref[1] * rows_own
    span = NPOW * LANES
    size = 2 * kx_own * rows_half
    scale = 1.0 / math.sqrt(NX * depth)
    kx = first_kx + lax.broadcasted_iota(jnp.int32, (kx_own, LANES), 0)
    theta = kx.astype(F32) * (2.0 * math.pi / NX)
    cosine = [None, jnp.cos(theta)]
    sine = [None, jnp.sin(theta)]
    for d in range(2, HALF + 1):
        cosine.append(cosine[-1] * cosine[1] - sine[-1] * sine[1])
        sine.append(sine[d - 1] * cosine[1] + cosine[d - 1] * sine[1])
    for d in range(1, HALF + 1):
        turn_ref[d - 1] = cosine[d]
        turn_ref[HALF + d - 1] = sine[d]
    total[...] = jnp.zeros_like(total)
    lhs_1[...] = jnp.zeros_like(lhs_1)
    rhs_1[...] = jnp.zeros_like(rhs_1)
    bins[:, 0] = jnp.zeros((2, FEAT, LANES), F32)
    most = tiles_ref[0, 55:56, :]
    for source in range(1, sources):
        most = jnp.maximum(most, tiles_ref[source, 55:56, :])
    most_ref[0] = jnp.max(most).astype(jnp.int32)
    ends = merge_sources(sources, tiles_ref, bins)
    lower = (ends[0] + LANES - 1) // LANES
    upper = jnp.maximum((ends[1] + LANES - 1) // LANES, 1)
    bins[1, upper] = jnp.zeros((FEAT, LANES), F32)

    def build(index, lhs, rhs, weights_x):
        half = (index >= lower).astype(jnp.int32)
        block = bins.at[half, index - half * lower]
        rate = -block[TERMS : TERMS + 1, :]
        centre_x = block[TERMS + 1 : TERMS + 2, :].astype(jnp.int32)
        centre_y = block[TERMS + 2 : TERMS + 3, :].astype(jnp.int32)
        centre_z = block[TERMS + 3 : TERMS + 4, :].astype(jnp.int32)
        even_0 = jnp.full((kx_own, LANES), 0.5 * scale, F32)
        even_2 = jnp.zeros((kx_own, LANES), F32)
        odd_1 = jnp.zeros((kx_own, LANES), F32)
        odd_3 = jnp.zeros((kx_own, LANES), F32)
        for d in range(1, HALF + 1):
            scaled = d / HALF
            weight = jnp.exp(rate * float(d * d)) * scale
            even = weight * turn_ref[d - 1]
            odd = (weight * scaled) * turn_ref[HALF + d - 1]
            even_0 = even_0 + even
            even_2 = even_2 + even * (scaled * scaled)
            odd_1 = odd_1 + odd
            odd_3 = odd_3 + odd * (scaled * scaled)
        phase = ((kx * centre_x) & (NX - 1)).astype(F32) * (2.0 * math.pi / NX)
        cos_c = jnp.cos(phase) * 2.0
        sin_c = jnp.sin(phase) * 2.0
        for second in range(NPOW):
            for third in range(NPOW):
                term = second * NPOW + third
                step = NPOW * NPOW
                even = block[term : term + 1, :] * even_0
                even = even + block[2 * step + term : 2 * step + term + 1, :] * even_2
                odd = block[step + term : step + term + 1, :] * odd_1
                odd = odd + block[3 * step + term : 3 * step + term + 1, :] * odd_3
                weights_x[term, 0:kx_own, :] = cos_c * even - sin_c * odd
                weights_x[term, kx_own:, :] = -(sin_c * even + cos_c * odd)
        shift_y = centre_y - (first_y + half * rows_half + NY // 2)
        y_cells = lax.broadcasted_iota(jnp.int32, (rows_half, LANES), 0)
        off_y = ((y_cells - shift_y) & (NY - 1)).astype(F32) - float(NY // 2)
        along_y = powers_of(off_y, rate)
        for third in range(NPOW):
            at = third * LANES
            for row in range(2 * kx_own):
                value = weights_x[third, row : row + 1, :] * along_y[0]
                for second in range(1, NPOW):
                    term = second * NPOW + third
                    value = value + weights_x[term, row : row + 1, :] * along_y[second]
                high, low = split(value)
                y_rows = slice(row * rows_half, (row + 1) * rows_half)
                lhs[y_rows, at : at + LANES] = high
                lhs[y_rows, span + at : span + at + LANES] = low
                lhs[y_rows, 2 * span + at : 2 * span + at + LANES] = high
        shift_z = centre_z - depth // 2
        z_cells = lax.broadcasted_iota(jnp.int32, (depth, LANES), 0)
        off_z = ((z_cells - shift_z) & (depth - 1)).astype(F32) - float(depth // 2)
        along_z = powers_of(off_z, rate)
        for third in range(NPOW):
            high, low = split(along_z[third])
            at = third * LANES
            rhs[:, at : at + LANES] = high
            rhs[:, span + at : span + at + LANES] = high
            rhs[:, 2 * span + at : 2 * span + at + LANES] = low

    def multiply(index, lhs, rhs):
        half = (index >= lower).astype(jnp.int32)
        total[half] += lax.dot_general(lhs[...], rhs[...], NT, preferred_element_type=F32)

    def two_blocks(pair, carry):
        multiply(2 * pair - 1, lhs_1, rhs_1)
        build(2 * pair, lhs_0, rhs_0, weights_0)
        multiply(2 * pair, lhs_0, rhs_0)
        build(2 * pair + 1, lhs_1, rhs_1, weights_1)
        return carry

    lax.fori_loop(0, (lower + upper + 1) // 2, two_blocks, 0)
    total[1] += lax.dot_general(lhs_1[...], rhs_1[...], NT, preferred_element_type=F32)
    copies = []
    for half in range(2):
        real_high, real_low = split(total[half, 0 : size // 2])
        imag_high, imag_low = split(total[half, size // 2 :])
        high = jnp.concatenate([real_high, imag_high], axis=1)
        low = jnp.concatenate([real_low, imag_low], axis=1)
        for part in range(2):
            columns = slice(part * depth, (part + 1) * depth)
            wave = wave_high_ref[:, columns]
            found = jnp.dot(high, wave, preferred_element_type=F32)
            found = found + jnp.dot(low, wave, preferred_element_type=F32)
            found = found + jnp.dot(high, wave_low_ref[:, columns], preferred_element_type=F32)
            stage[half, part] = found.reshape(kx_own, rows_half, depth)
            copies.append(
                pltpu.make_async_copy(
                    stage.at[half, part],
                    out_ref.at[part, :, half * rows_half : (half + 1) * rows_half, :],
                    sems.at[half, part],
                )
            )
            copies[-1].start()
    for copy in copies:
        copy.wait()


def spectrum_of(sources, groups, kx_own, depth, place, tiles, wave_high, wave_low):
    rows_own = NY // groups
    rows_half = rows_own // 2
    size = 2 * kx_own * rows_half
    span = 3 * NPOW * LANES
    columns = sources * SLOTS // LANES + 2
    vmem = pl.BlockSpec(memory_space=pltpu.VMEM)
    smem = pl.BlockSpec(memory_space=pltpu.SMEM)
    return pl.pallas_call(
        functools.partial(spectrum_kernel, sources, groups, kx_own, depth),
        in_specs=[smem, vmem, vmem, vmem],
        out_specs=[pl.BlockSpec(memory_space=pltpu.HBM), smem],
        out_shape=[
            jax.ShapeDtypeStruct((2, kx_own, rows_own, depth), F32),
            jax.ShapeDtypeStruct((1,), jnp.int32),
        ],
        scratch_shapes=[
            pltpu.VMEM((2, columns, FEAT, LANES), F32),
            pltpu.VMEM((2, size, depth), F32),
            pltpu.VMEM((size, span), BF16),
            pltpu.VMEM((size, span), BF16),
            pltpu.VMEM((depth, span), BF16),
            pltpu.VMEM((depth, span), BF16),
            pltpu.VMEM((NPOW * NPOW, 2 * kx_own, LANES), F32),
            pltpu.VMEM((NPOW * NPOW, 2 * kx_own, LANES), F32),
            pltpu.VMEM((2 * HALF, kx_own, LANES), F32),
            pltpu.VMEM((2, 2, kx_own, rows_half, depth), F32),
            pltpu.SemaphoreType.DMA((2, 2)),
        ],
        compiler_params=pltpu.CompilerParams(vmem_limit_bytes=40 * 2**20),
        name="spectrum_of_tiles",
    )(place, tiles, wave_high, wave_low)


def wave_table(depth):
    cells = np.arange(depth)
    angle = 2.0 * np.pi * (cells[:, None] * cells[None, :] % depth) / depth
    cosine, sine = np.cos(angle), np.sin(angle)
    table = np.block([[cosine, -sine], [sine, cosine]]).astype(np.float32)
    high = table.astype(jnp.bfloat16)
    low = (table - high.astype(np.float32)).astype(jnp.bfloat16)
    return high, low


def exchange(value, groups):
    return lax.all_to_all(
        value, ("slab", "grp"), split_axis=0, concat_axis=0, tiled=True, axis_index_groups=groups
    )


def local(tile_centres, tile_coeffs, tile_exponents, tile_live):
    slab_count = lax.axis_size("slab")
    grp_count = lax.axis_size("grp")
    slab, grp = lax.axis_index("slab"), lax.axis_index("grp")
    depth = CZ * slab_count
    kx_own = NX // 2 // slab_count
    count_z = slab_count // COUNT_X
    count_y = grp_count // 2

    def device(x, z, y, core):
        return (x * count_z + z) * grp_count + y * 2 + core

    xs, zs, ys, cores = range(COUNT_X), range(count_z), range(count_y), range(2)
    share = [[device(x, z, y, c) for z in zs for c in cores] for x in xs for y in ys]
    spread = [[device(x, z, y, c) for x in xs for y in ys] for z in zs for c in cores]
    sharers, chunks = len(share[0]), len(spread[0])
    place = jnp.stack([slab, grp]).astype(jnp.int32)
    wave_high, wave_low = (jnp.asarray(part) for part in wave_table(depth))
    tri = jnp.asarray(np.triu(np.ones((256, 256), np.float32), 1).astype(jnp.bfloat16))
    packed = pack_tiles(sharers, tile_centres, tile_coeffs, tile_exponents, tile_live)
    tiles = exchange(packed.reshape(sharers, 1, ROWS * LANES), share).reshape(sharers * ROWS, LANES)

    def one_round(index):
        scalars = jnp.stack([index, grp % 2]).astype(jnp.int32)
        routed = route_tiles(sharers, chunks, grp_count, tri, scalars, tiles)
        routed = exchange(routed.reshape(chunks, BLOCK, LANES), spread)
        return spectrum_of(chunks, grp_count, kx_own, depth, place, routed, wave_high, wave_low)

    found, most = one_round(jnp.int32(0))

    def more(state):
        return state[0] * SLOTS < state[1]

    def again(state):
        index, most, found = state
        return index + 1, most, found + one_round(index)[0]

    return lax.while_loop(more, again, (jnp.int32(1), most[0], found))[2]


def solution(mesh):
    return jax.shard_map(
        local,
        mesh=mesh,
        in_specs=(
            P(None, ("slab", "grp")),
            P(None, ("slab", "grp")),
            P(("slab", "grp")),
            P(("slab", "grp")),
        ),
        out_specs=P(None, "slab", "grp", None),
        check_vma=False,
    )
```

profile of v0, /device:TPU:1, one launch (start us, length us, event | category | flops | bytes accessed | tf_op | source)
XLA Modules:
  0.0 55.5 jit_solution(327253330819531078)
XLA Ops:
  0.0 1.5 %pack_tiles.1 = f32[272,128]{1,0:T(8,128)} custom-call(f32[32,64]{1,0:T(8,128)} %bitcast.24, s32[3,32]{1,0:T(4,128)} %centres_ref.1, f32[1,32]{1,0:T(1,128)} %bitcast.25, s32[1,32]{1,0:T(1,128)} %bitcast.26), custom_call_target="tpu_custom_call" | custom-call | tf_op jit(solution)/shard_map/pack_tiles/pallas_call | solution.py:51
  1.5 10.0 %all-to-all-start.1 = ((f32[16,1,2176]{2,1,0:T(1,128)}), f32[16,1,2176]{2,1,0:T(1,128)S(1)}, u32[]{:S(2)}, u32[]{:S(2)}) async-start(f32[16,1,2176]{2,1,0:T(1,128)} %bitcast.23), calls=%async_computation.1 | async-start | bytes 278528 | tf_op jit(solution)/shard_map/all_to_all | solution.py:383
  11.5 0.6 %pad_add_fusion.2.scalar_ref = s32[2]{0:T(128)} fusion(s32[1]{0:T(128)} %bitcast.2, s32[1]{0:T(128)} %constant.50.clone.1), kind=kLoop, calls=%fused_computation.2 | loop fusion | flops 2 | bytes 16 | tf_op jit(solution)/shard_map/stack | solution.py:411
  12.1 8.5 %all-to-all-done.1 = f32[16,1,2176]{2,1,0:T(1,128)S(1)} async-done(((f32[16,1,2176]{2,1,0:T(1,128)}), f32[16,1,2176]{2,1,0:T(1,128)S(1)}, u32[]{:S(2)}, u32[]{:S(2)}) %all-to-all-start.1) | async-done | bytes 139296 | tf_op jit(solution)/shard_map/all_to_all | solution.py:383
  20.5 0.0 copy-start.1
  20.5 2.5 %route_tiles.4 = f32[896,128]{1,0:T(8,128)} custom-call(bf16[256,256]{1,0:T(8,128)(2,1)} %constant.55.clone.tri_ref, s32[2]{0:T(128)} %pad_add_fusion.2.scalar_ref, f32[272,128]{1,0:T(8,128)S(1)} %bitcast.20), custom_call_target="tpu_custom_call" | custom-call | tf_op jit(solution)/shard_map/route_tiles/pallas_call | solution.py:144
  23.0 0.0 copy-start
  23.0 6.9 %all-to-all-start.2 = ((f32[16,56,128]{2,1,0:T(8,128)}), f32[16,56,128]{2,1,0:T(8,128)S(1)}, u32[]{:S(2)}, u32[]{:S(2)}) async-start(f32[16,56,128]{2,1,0:T(8,128)} %bitcast.22), calls=%async_computation.2 | async-start | bytes 917504 | tf_op jit(solution)/shard_map/all_to_all | solution.py:383
  29.9 0.1 pad_add_fusion.1.place_ref
  30.0 0.0 copy-start.3
  30.0 0.0 copy-start.5
  30.0 9.5 %all-to-all-done.2.tiles_ref = f32[16,56,128]{2,1,0:T(8,128)S(1)} async-done(((f32[16,56,128]{2,1,0:T(8,128)}), f32[16,56,128]{2,1,0:T(8,128)S(1)}, u32[]{:S(2)}, u32[]{:S(2)}) %all-to-all-start.2) | async-done | bytes 458784 | tf_op jit(solution)/shard_map/all_to_all | solution.py:383
  39.5 0.0 copy-done.1
  39.5 0.0 copy-done
  39.5 14.3 %spectrum_of_tiles.4 = (f32[2,8,64,256]{3,2,1,0:T(8,128)S(1)}, s32[1]{0:T(128)}) custom-call(s32[2]{0:T(128)S(1)} %pad_add_fusion.1.place_ref, f32[16,56,128]{2,1,0:T(8,128)S(1)} %all-to-all-done.2.tiles_ref, bf16[512,512]{1,0:T(8,128)(2,1)S(1)} %copy-done.1, bf16[512,512]{1,0:T(8,128)(2,1)S(1)} %copy-done), custom_call_target="tpu_custom_call" | custom-call | tf_op jit(solution)/shard_map/spectrum_of_tiles/pallas_call | solution.py:346
  53.9 0.0 copy-done.3
  53.9 0.0 copy-done.5
  53.9 0.6 %while.13 = (s32[]{:T(128)}, f32[2,8,64,256]{3,2,1,0:T(8,128)S(1)}, s32[]{:T(128)}, s32[]{:T(128)}, f32[272,128]{1,0:T(8,128)S(1)}, /*index=5*/s32[2]{0:T(128)S(...) while((s32[]{:T(128)}, f32[2,8,64,256]{3,2,1,0:T(8,128)S(1)}, ...), condition=%wide.region_1.2_spmd.clone, body=%wide.region_0.1_spmd.sunk.clone.sunk | while | flops 262149 | bytes 6619325 | solution.py:425
  54.5 0.0 copy-start.2
  54.5 1.0 %copy-done.2 = f32[2,8,64,256]{3,2,1,0:T(8,128)} copy-done((f32[2,8,64,256]{3,2,1,0:T(8,128)}, f32[2,8,64,256]{3,2,1,0:T(8,128)S(1)}, u32[]{:S(2)}) %copy-start.2) | copy-done | bytes 1048600
Async XLA Ops:
  1.5 19.0 %all-to-all-start.1 = ((f32[16,1,2176]{2,1,0:T(1,128)}), f32[16,1,2176]{2,1,0:T(1,128)S(1)}, u32[]{:S(2)}, u32[]{:S(2)}) async-start(f32[16,1,2176]{2,1,0:T(1,128)} %bitcast.23), calls=%async_computation.1 | async-start | bytes 278528 | tf_op jit(solution)/shard_map/all_to_all | solution.py:383
  20.5 19.0 %copy-start.1 = (bf16[512,512]{1,0:T(8,128)(2,1)S(1)}, bf16[512,512]{1,0:T(8,128)(2,1)}, u32[]{:S(2)}) copy-start(bf16[512,512]{1,0:T(8,128)(2,1)} %constant.53.clone.wave_high_ref) | copy-start | bytes 1572868
  23.0 16.5 %copy-start = (bf16[512,512]{1,0:T(8,128)(2,1)S(1)}, bf16[512,512]{1,0:T(8,128)(2,1)}, u32[]{:S(2)}) copy-start(bf16[512,512]{1,0:T(8,128)(2,1)} %constant.54.clone.wave_low_ref) | copy-start | bytes 1572868
  23.0 16.5 %all-to-all-start.2 = ((f32[16,56,128]{2,1,0:T(8,128)}), f32[16,56,128]{2,1,0:T(8,128)S(1)}, u32[]{:S(2)}, u32[]{:S(2)}) async-start(f32[16,56,128]{2,1,0:T(8,128)} %bitcast.22), calls=%async_computation.2 | async-start | bytes 917504 | tf_op jit(solution)/shard_map/all_to_all | solution.py:383
  30.0 23.9 %copy-start.3 = (bf16[512,512]{1,0:T(8,128)(2,1)S(1)}, bf16[512,512]{1,0:T(8,128)(2,1)}, u32[]{:S(2)}) copy-start(bf16[512,512]{1,0:T(8,128)(2,1)} %constant.54.clone..sunk.2) | copy-start | bytes 1572868
  30.0 23.9 %copy-start.5 = (bf16[256,256]{1,0:T(8,128)(2,1)S(1)}, bf16[256,256]{1,0:T(8,128)(2,1)}, u32[]{:S(2)}) copy-start(bf16[256,256]{1,0:T(8,128)(2,1)} %constant.55.clone..sunk.2) | copy-start | bytes 393220
  54.5 1.0 %copy-start.2 = (f32[2,8,64,256]{3,2,1,0:T(8,128)}, f32[2,8,64,256]{3,2,1,0:T(8,128)S(1)}, u32[]{:S(2)}) copy-start(f32[2,8,64,256]{3,2,1,0:T(8,128)S(1)} %get-tuple-element.235) | copy-start | bytes 3145732
where the time goes:
time: 55.8 us; the launch traced here: 55.5 us
  Pallas kernels  18.3 us (33%)
  waiting for transfers between devices  18 us (32%)
  starting transfers between devices  16.9 us (30%)
  local copies, waits for them, and re-layouts  0.98 us (2%)
  other arithmetic  0.68 us (1%)
  loops' own time  0.63 us (1%)
    all_to_all x2, waiting for transfers between devices, exchange(): lax.all_to_all(value, ('slab', 'grp'), split_axis=0, concat_axis=0, tiled...  18 us
    all_to_all x2, starting transfers between devices, exchange(): lax.all_to_all(value, ('slab', 'grp'), split_axis=0, concat_axis=0, tiled...  16.9 us
    pallas_call x1, Pallas kernels, spectrum_of(): pl.pallas_call(functools.partial(spectrum_kernel, sources, groups, kx_own...  14.3 us
    pallas_call x1, Pallas kernels, route_tiles(): pl.pallas_call(functools.partial(route_kernel, sources, groups), in_specs...  2.46 us
    pallas_call x1, Pallas kernels, pack_tiles(): pl.pallas_call(functools.partial(pack_kernel, copies), out_shape=jax.Shap...  1.49 us
  transfers between devices with their start and end apart: 2, of which 2 were waited for; matrix products, arithmetic and copies ran while one was open for 1% of the time, Pallas kernels for 0%

commit v1 on v0

--- a/solution.py
+++ b/solution.py
@@ -31,7 +31,7 @@
     return high, (value - high.astype(F32)).astype(BF16)
 
 
-def pack_kernel(copies, coeffs_ref, centres_ref, exponents_ref, live_ref, out_ref, block):
+def pack_kernel(copies, place_ref, coeffs_ref, centres_ref, exponents_ref, live_ref, out_ref, block):
     half = coeffs_ref.shape[0] // 2
     block[0:half, 0:TERMS] = coeffs_ref[0:half, :]
     block[0:half, TERMS:] = coeffs_ref[half:, :]
@@ -47,16 +47,19 @@
         out_ref[copy * ROWS : (copy + 1) * ROWS, :] = value
 
 
-def pack_tiles(copies, tile_centres, tile_coeffs, tile_exponents, tile_live):
+def pack_tiles(copies, place, tile_centres, tile_coeffs, tile_exponents, tile_live):
+    vmem = pl.BlockSpec(memory_space=pltpu.VMEM)
     return pl.pallas_call(
         functools.partial(pack_kernel, copies),
+        in_specs=[pl.BlockSpec(memory_space=pltpu.SMEM), vmem, vmem, vmem, vmem],
+        out_specs=vmem,
         out_shape=jax.ShapeDtypeStruct((copies * ROWS, LANES), F32),
         scratch_shapes=[pltpu.VMEM((ROWS, LANES), F32)],
         name="pack_tiles",
-    )(tile_coeffs.T, tile_centres, tile_exponents[None, :], tile_live[None, :])
-
-
-def route_kernel(sources, groups, tri_ref, scalar_ref, tiles_ref, out_ref, rows_ref, table, rank_ref, count_ref):
+    )(place, tile_coeffs.T, tile_centres, tile_exponents[None, :], tile_live[None, :])
+
+
+def route_kernel(sources, groups, place_ref, round_ref, tiles_ref, out_ref, rows_ref, table, rank_ref, count_ref):
     per_row = 16
     side = sources * per_row
     total = 2 * side
@@ -88,8 +91,9 @@
     reach = (centre_y - group * rows_own + HALF) & (NY - 1)
     reach = jnp.where(centre_y >= 0, reach, NY)
     edges = (0, rows_own // 2, rows_own // 2 + 2 * HALF, rows_own + 2 * HALF)
-    tri = tri_ref[...]
-    step = tri.shape[0]
+    step = 256
+    earlier = lax.broadcasted_iota(jnp.int32, (step, step), 0) < lax.broadcasted_iota(jnp.int32, (step, step), 1)
+    tri = jnp.where(earlier, 1.0, 0.0).astype(BF16)
     marks = []
     for kind in range(3):
         inside = jnp.where((reach >= edges[kind]) & (reach < edges[kind + 1]), 1.0, 0.0)
@@ -107,8 +111,8 @@
             count = count + jnp.sum(marks[index], axis=1, keepdims=True)
             index += 1
         count_ref[kind] = jnp.broadcast_to(count, (groups, LANES))
-    base = (scalar_ref[0] * SLOTS).astype(F32)
-    core = scalar_ref[1]
+    base = (round_ref[0] * SLOTS).astype(F32)
+    core = place_ref[1] % 2
     high, low = split(table[...])
     both = jnp.concatenate([high, low], axis=0)
     depth = table.shape[0]
@@ -140,11 +144,11 @@
             out_ref[at + 48 : at + 56, :] = numbers
 
 
-def route_tiles(sources, targets, groups, tri, scalars, tiles):
+def route_tiles(sources, targets, groups, place, round_index, tiles):
     return pl.pallas_call(
         functools.partial(route_kernel, sources, groups),
         in_specs=[
-            pl.BlockSpec(memory_space=pltpu.VMEM),
+            pl.BlockSpec(memory_space=pltpu.SMEM),
             pl.BlockSpec(memory_space=pltpu.SMEM),
             pl.BlockSpec(memory_space=pltpu.VMEM),
         ],
@@ -157,7 +161,7 @@
             pltpu.VMEM((3, groups, LANES), F32),
         ],
         name="route_tiles",
-    )(tri, scalars, tiles)
+    )(place, round_index, tiles)
 
 
 def powers_of(distance, rate):
@@ -172,46 +176,85 @@
 
 def merge_sources(sources, tiles_ref, bins):
     lane = lax.broadcasted_iota(jnp.int32, (8, LANES), 1)
+    first = LANES // 2
+    counts = [tiles_ref[pl.ds(52 + k, sources, stride=BLOCK), :] for k in range(3)]
     ends = [jnp.int32(0), jnp.int32(0)]
+    open_column = [[jnp.zeros((8, LANES), F32)] * (FEAT // 8) for _ in range(2)]
     for source in range(sources):
-        block = tiles_ref.at[source]
         held, upto, start = (
-            jnp.max(block[52 + k : 53 + k, :]).astype(jnp.int32) for k in range(3)
+            jnp.max(count[source : source + 1, :]).astype(jnp.int32) for count in counts
         )
-        pieces = []
-        for row in range(0, 32, 8):
-            extra = block[32 + row % 16 : 40 + row % 16, :]
-            pieces.append(
-                jnp.where(lane < 64, block[row : row + 8, :], pltpu.roll(extra, 64 if row < 16 else 32, 1))
-            )
-        for row in range(0, 32, 8):
-            extra = block[32 + row % 16 : 40 + row % 16, :]
-            extra = extra if row < 16 else pltpu.roll(extra, 96, 1)
-            pieces.append(jnp.where(lane < 64, pltpu.roll(block[row : row + 8, :], 64, 1), extra))
-        pieces.append(block[48:56, :])
+        at = source * BLOCK
+        pieces = [tiles_ref[at + row : at + row + 8, :] for row in range(0, 32, 8)]
+        numbers = tiles_ref[at + 48 : at + 56, :]
         for half, (begin, end) in enumerate(((jnp.int32(0), upto), (start, held))):
-            valid = (lane >= begin) & (lane < end)
+            begin, end = jnp.minimum(begin, first), jnp.minimum(end, first)
             column = ends[half] // LANES
             offset = ends[half] % LANES
             shift = (offset - begin + LANES) % LANES
-            for part, piece in enumerate(pieces):
-                moved = pltpu.roll(jnp.where(valid, piece, 0.0), shift, 1)
-                rows = slice(8 * part, 8 * part + 8)
-                bins[half, column, rows, :] = jnp.where(lane < offset, bins[half, column, rows, :], moved)
-                bins[half, column + 1, rows, :] = jnp.where(lane < offset, moved, 0.0)
-            ends[half] = ends[half] + (end - begin)
-    return ends
+            after = ends[half] + (end - begin)
+            kept = lane < offset
+            stays = after // LANES == column
+            lower = (lane >= begin) & (lane < end)
+            upper = (lane >= begin + first) & (lane < end + first)
+            other = (shift + first) % LANES
+            moved = [pltpu.roll(jnp.where(lower, piece, 0.0), shift, 1) for piece in pieces]
+            moved += [pltpu.roll(jnp.where(upper, piece, 0.0), other, 1) for piece in pieces]
+            moved.append(pltpu.roll(jnp.where(lower, numbers, 0.0), shift, 1))
+            for part, piece in enumerate(moved):
+                full = jnp.where(kept, open_column[half][part], piece)
+                bins[half, column, 8 * part : 8 * part + 8, :] = full
+                wrapped = jnp.where(kept, piece, 0.0)
+                open_column[half][part] = jnp.where(stays, full, wrapped)
+            ends[half] = after
+    for half in range(2):
+        for part in range(FEAT // 8):
+            bins[half, ends[half] // LANES, 8 * part : 8 * part + 8, :] = open_column[half][part]
+
+    def rest(source, ends):
+        at = pl.multiple_of(source * BLOCK, 8)
+        numbers = tiles_ref[pl.ds(at + 48, 8), :]
+        held, upto, start = (jnp.max(numbers[4 + k : 5 + k]).astype(jnp.int32) for k in range(3))
+
+        def append(ends):
+            lines = [tiles_ref[pl.ds(at + 32 + row, 8), :] for row in (0, 8)]
+            result = []
+            for half, (begin, end) in enumerate(((jnp.int32(0), upto), (start, held))):
+                begin, end = jnp.maximum(begin, first) - first, jnp.maximum(end, first) - first
+                column = ends[half] // LANES
+                offset = ends[half] % LANES
+                kept = lane < offset
+                moved = []
+                for quarter in range(4):
+                    valid = (lane >= begin + 32 * quarter) & (lane < end + 32 * quarter)
+                    shift = (offset - begin - 32 * quarter + 2 * LANES) % LANES
+                    moved += [pltpu.roll(jnp.where(valid, line, 0.0), shift, 1) for line in lines]
+                valid = (lane >= begin + first) & (lane < end + first)
+                shift = (offset - begin - first + 2 * LANES) % LANES
+                moved.append(pltpu.roll(jnp.where(valid, numbers, 0.0), shift, 1))
+                for part, piece in enumerate(moved):
+                    rows = slice(8 * part, 8 * part + 8)
+                    bins[half, column, rows, :] = jnp.where(kept, bins[half, column, rows, :], piece)
+                    bins[half, column + 1, rows, :] = jnp.where(kept, piece, 0.0)
+                result.append(ends[half] + end - begin)
+            return tuple(result)
+
+        return lax.cond(held > first, append, lambda ends: ends, ends)
+
+    return lax.fori_loop(0, sources, rest, tuple(ends))
 
 
 def spectrum_kernel(
-    sources, groups, kx_own, depth, place_ref, tiles_ref, wave_high_ref, wave_low_ref,
-    out_ref, most_ref, bins, total, lhs_0, lhs_1, rhs_0, rhs_1, weights_0, weights_1, turn_ref, stage, sems,
+    sources, groups, kx_own, depth, later, place_ref, tiles_ref, wave, *refs
 ):
+    if later:
+        before_ref, *refs = refs
+    out_ref, most_ref, bins, total, *refs = refs
+    lhs_0, lhs_1, rhs_0, rhs_1, weights_0, weights_1, turn_ref, stage, sems = refs
     rows_own = NY // groups
     rows_half = rows_own // 2
     first_kx = place_ref[0] * kx_own
     first_y = place_ref[1] * rows_own
-    span = NPOW * LANES
     size = 2 * kx_own * rows_half
     scale = 1.0 / math.sqrt(NX * depth)
     kx = first_kx + lax.broadcasted_iota(jnp.int32, (kx_own, LANES), 0)
@@ -227,15 +270,11 @@
     total[...] = jnp.zeros_like(total)
     lhs_1[...] = jnp.zeros_like(lhs_1)
     rhs_1[...] = jnp.zeros_like(rhs_1)
-    bins[:, 0] = jnp.zeros((2, FEAT, LANES), F32)
-    most = tiles_ref[0, 55:56, :]
-    for source in range(1, sources):
-        most = jnp.maximum(most, tiles_ref[source, 55:56, :])
-    most_ref[0] = jnp.max(most).astype(jnp.int32)
+    most_ref[0] = jnp.max(tiles_ref[pl.ds(55, sources, stride=BLOCK), :]).astype(jnp.int32)
+    most_ref[1] = jnp.int32(1)
     ends = merge_sources(sources, tiles_ref, bins)
     lower = (ends[0] + LANES - 1) // LANES
     upper = jnp.maximum((ends[1] + LANES - 1) // LANES, 1)
-    bins[1, upper] = jnp.zeros((FEAT, LANES), F32)
 
     def build(index, lhs, rhs, weights_x):
         half = (index >= lower).astype(jnp.int32)
@@ -275,7 +314,6 @@
         off_y = ((y_cells - shift_y) & (NY - 1)).astype(F32) - float(NY // 2)
         along_y = powers_of(off_y, rate)
         for third in range(NPOW):
-            at = third * LANES
             for row in range(2 * kx_own):
                 value = weights_x[third, row : row + 1, :] * along_y[0]
                 for second in range(1, NPOW):
@@ -283,23 +321,26 @@
                     value = value + weights_x[term, row : row + 1, :] * along_y[second]
                 high, low = split(value)
                 y_rows = slice(row * rows_half, (row + 1) * rows_half)
-                lhs[y_rows, at : at + LANES] = high
-                lhs[y_rows, span + at : span + at + LANES] = low
-                lhs[y_rows, 2 * span + at : 2 * span + at + LANES] = high
+                lhs[third, y_rows, :] = high
+                lhs[NPOW + third, y_rows, :] = low
         shift_z = centre_z - depth // 2
         z_cells = lax.broadcasted_iota(jnp.int32, (depth, LANES), 0)
         off_z = ((z_cells - shift_z) & (depth - 1)).astype(F32) - float(depth // 2)
         along_z = powers_of(off_z, rate)
         for third in range(NPOW):
             high, low = split(along_z[third])
-            at = third * LANES
-            rhs[:, at : at + LANES] = high
-            rhs[:, span + at : span + at + LANES] = high
-            rhs[:, 2 * span + at : 2 * span + at + LANES] = low
+            rhs[third] = high
+            rhs[NPOW + third] = low
+
+    def product(lhs, rhs):
+        highs, lows = range(NPOW), range(NPOW, 2 * NPOW)
+        left = jnp.concatenate([lhs[k] for k in (*highs, *lows, *highs)], axis=1)
+        right = jnp.concatenate([rhs[k] for k in (*highs, *highs, *lows)], axis=1)
+        return lax.dot_general(left, right, NT, preferred_element_type=F32)
 
     def multiply(index, lhs, rhs):
         half = (index >= lower).astype(jnp.int32)
-        total[half] += lax.dot_general(lhs[...], rhs[...], NT, preferred_element_type=F32)
+        total[half] += product(lhs, rhs)
 
     def two_blocks(pair, carry):
         multiply(2 * pair - 1, lhs_1, rhs_1)
@@ -308,65 +349,76 @@
         build(2 * pair + 1, lhs_1, rhs_1, weights_1)
         return carry
 
-    lax.fori_loop(0, (lower + upper + 1) // 2, two_blocks, 0)
-    total[1] += lax.dot_general(lhs_1[...], rhs_1[...], NT, preferred_element_type=F32)
-    copies = []
+    blocks = lower + upper
+    lax.fori_loop(0, blocks // 2, two_blocks, 0)
+    @pl.when(blocks % 2 == 0)
+    def _():
+        total[1] += product(lhs_1, rhs_1)
+
+    @pl.when(blocks % 2 == 1)
+    def _():
+        multiply(blocks - 2, lhs_1, rhs_1)
+        build(blocks - 1, lhs_0, rhs_0, weights_0)
+        total[1] += product(lhs_0, rhs_0)
+
+    parts = []
     for half in range(2):
         real_high, real_low = split(total[half, 0 : size // 2])
         imag_high, imag_low = split(total[half, size // 2 :])
         high = jnp.concatenate([real_high, imag_high], axis=1)
         low = jnp.concatenate([real_low, imag_low], axis=1)
-        for part in range(2):
-            columns = slice(part * depth, (part + 1) * depth)
-            wave = wave_high_ref[:, columns]
-            found = jnp.dot(high, wave, preferred_element_type=F32)
-            found = found + jnp.dot(low, wave, preferred_element_type=F32)
-            found = found + jnp.dot(high, wave_low_ref[:, columns], preferred_element_type=F32)
-            stage[half, part] = found.reshape(kx_own, rows_half, depth)
-            copies.append(
-                pltpu.make_async_copy(
-                    stage.at[half, part],
-                    out_ref.at[part, :, half * rows_half : (half + 1) * rows_half, :],
-                    sems.at[half, part],
-                )
-            )
-            copies[-1].start()
-    for copy in copies:
-        copy.wait()
-
-
-def spectrum_of(sources, groups, kx_own, depth, place, tiles, wave_high, wave_low):
+        parts.append((high, low))
+    for part in range(2):
+        if later:
+            pltpu.sync_copy(before_ref.at[part], stage.at[part])
+        columns = slice(part * depth, (part + 1) * depth)
+        for half, (high, low) in enumerate(parts):
+            found = jnp.dot(high, wave[0, :, columns], preferred_element_type=F32)
+            found = found + jnp.dot(low, wave[0, :, columns], preferred_element_type=F32)
+            found = found + jnp.dot(high, wave[1, :, columns], preferred_element_type=F32)
+            found = found.reshape(kx_own, rows_half, depth)
+            rows = slice(half * rows_half, (half + 1) * rows_half)
+            if later:
+                found = found + stage[part, :, rows, :]
+            stage[part, :, rows, :] = found
+        pltpu.make_async_copy(stage.at[part], out_ref.at[part], sems.at[part]).start()
+    for part in range(2):
+        pltpu.make_async_copy(stage.at[part], out_ref.at[part], sems.at[part]).wait()
+
+
+def spectrum_of(sources, groups, kx_own, depth, place, tiles, wave, before=None):
     rows_own = NY // groups
-    rows_half = rows_own // 2
-    size = 2 * kx_own * rows_half
-    span = 3 * NPOW * LANES
+    size = kx_own * rows_own
     columns = sources * SLOTS // LANES + 2
     vmem = pl.BlockSpec(memory_space=pltpu.VMEM)
     smem = pl.BlockSpec(memory_space=pltpu.SMEM)
+    hbm = pl.BlockSpec(memory_space=pltpu.HBM)
+    later = before is not None
     return pl.pallas_call(
-        functools.partial(spectrum_kernel, sources, groups, kx_own, depth),
-        in_specs=[smem, vmem, vmem, vmem],
-        out_specs=[pl.BlockSpec(memory_space=pltpu.HBM), smem],
+        functools.partial(spectrum_kernel, sources, groups, kx_own, depth, later),
+        in_specs=[smem, vmem, vmem] + [hbm] * later,
+        out_specs=[hbm, smem],
         out_shape=[
             jax.ShapeDtypeStruct((2, kx_own, rows_own, depth), F32),
-            jax.ShapeDtypeStruct((1,), jnp.int32),
+            jax.ShapeDtypeStruct((2,), jnp.int32),
         ],
+        input_output_aliases={3: 0} if later else {},
         scratch_shapes=[
             pltpu.VMEM((2, columns, FEAT, LANES), F32),
             pltpu.VMEM((2, size, depth), F32),
-            pltpu.VMEM((size, span), BF16),
-            pltpu.VMEM((size, span), BF16),
-            pltpu.VMEM((depth, span), BF16),
-            pltpu.VMEM((depth, span), BF16),
+            pltpu.VMEM((2 * NPOW, size, LANES), BF16),
+            pltpu.VMEM((2 * NPOW, size, LANES), BF16),
+            pltpu.VMEM((2 * NPOW, depth, LANES), BF16),
+            pltpu.VMEM((2 * NPOW, depth, LANES), BF16),
             pltpu.VMEM((NPOW * NPOW, 2 * kx_own, LANES), F32),
             pltpu.VMEM((NPOW * NPOW, 2 * kx_own, LANES), F32),
             pltpu.VMEM((2 * HALF, kx_own, LANES), F32),
-            pltpu.VMEM((2, 2, kx_own, rows_half, depth), F32),
-            pltpu.SemaphoreType.DMA((2, 2)),
+            pltpu.VMEM((2, kx_own, rows_own, depth), F32),
+            pltpu.SemaphoreType.DMA((2,)),
         ],
         compiler_params=pltpu.CompilerParams(vmem_limit_bytes=40 * 2**20),
         name="spectrum_of_tiles",
-    )(place, tiles, wave_high, wave_low)
+    )(place, tiles, wave, *([before] if later else []))
 
 
 def wave_table(depth):
@@ -376,7 +428,7 @@
     table = np.block([[cosine, -sine], [sine, cosine]]).astype(np.float32)
     high = table.astype(jnp.bfloat16)
     low = (table - high.astype(np.float32)).astype(jnp.bfloat16)
-    return high, low
+    return np.stack([high, low])
 
 
 def exchange(value, groups):
@@ -402,16 +454,14 @@
     spread = [[device(x, z, y, c) for x in xs for y in ys] for z in zs for c in cores]
     sharers, chunks = len(share[0]), len(spread[0])
     place = jnp.stack([slab, grp]).astype(jnp.int32)
-    wave_high, wave_low = (jnp.asarray(part) for part in wave_table(depth))
-    tri = jnp.asarray(np.triu(np.ones((256, 256), np.float32), 1).astype(jnp.bfloat16))
-    packed = pack_tiles(sharers, tile_centres, tile_coeffs, tile_exponents, tile_live)
+    wave = jnp.asarray(wave_table(depth))
+    packed = pack_tiles(sharers, place, tile_centres, tile_coeffs, tile_exponents, tile_live)
     tiles = exchange(packed.reshape(sharers, 1, ROWS * LANES), share).reshape(sharers * ROWS, LANES)
 
-    def one_round(index):
-        scalars = jnp.stack([index, grp % 2]).astype(jnp.int32)
-        routed = route_tiles(sharers, chunks, grp_count, tri, scalars, tiles)
-        routed = exchange(routed.reshape(chunks, BLOCK, LANES), spread)
-        return spectrum_of(chunks, grp_count, kx_own, depth, place, routed, wave_high, wave_low)
+    def one_round(index, before=None):
+        routed = route_tiles(sharers, chunks, grp_count, place, index.reshape(1), tiles)
+        routed = exchange(routed.reshape(chunks, BLOCK, LANES), spread).reshape(chunks * BLOCK, LANES)
+        return spectrum_of(chunks, grp_count, kx_own, depth, place, routed, wave, before)
 
     found, most = one_round(jnp.int32(0))
 
@@ -420,9 +470,9 @@
 
     def again(state):
         index, most, found = state
-        return index + 1, most, found + one_round(index)[0]
-
-    return lax.while_loop(more, again, (jnp.int32(1), most[0], found))[2]
+        return index + 1, most, one_round(index, found)[0]
+
+    return lax.while_loop(more, again, (most[1], most[0], found))[2]
 
 
 def solution(mesh):

time: 55.8 us -> 57.3 us (1.027)
  blocking collectives: 0 us -> 35.5 us
  waiting for transfers between devices: 18 us -> 0 us
  starting transfers between devices: 16.9 us -> 0 us
  loops' own time: 0.63 us -> 1.49 us
  local copies, waits for them, and re-layouts: 0.98 us -> 1.61 us
  other arithmetic: 0.68 us -> 0.07 us
    all_to_all x0 -> x2, blocking collectives: none -> 35.5 us  [exchange(): lax.all_to_all(value, ('slab', 'grp'), split_axis=0, concat_axis=0, tiled...]
    all_to_all x2 -> x0, waiting for transfers between devices: 18 us -> none  [exchange(): lax.all_to_all(value, ('slab', 'grp'), split_axis=0, concat_axis=0, tiled...]
    all_to_all x2 -> x0, starting transfers between devices: 16.9 us -> none  [exchange(): lax.all_to_all(value, ('slab', 'grp'), split_axis=0, concat_axis=0, tiled...]
    another operation x1, loops' own time: 0.63 us -> 1.49 us  [local(): return lax.while_loop(more, again, (most[1], most[0], found))[2]]
    slice x0 -> x1, local copies, waits for them, and re-layouts: none -> 0.63 us  [local(): return lax.while_loop(more, again, (most[1], most[0], found))[2]]
    another operation x1 -> x0, other arithmetic: 0.61 us -> none  [one_round(): scalars = jnp.stack([index, grp % 2]).astype(jnp.int32)]
  transfers between devices with their start and end apart: 2 -> 0, of which waited for: 2 -> 0; matrix products, arithmetic and copies ran while one was open for 1% -> 0% of each run, Pallas kernels for 0% -> 0%
where the time goes in v1:
time: 57.3 us; the launch traced here: 56.9 us
  blocking collectives  35.5 us (62%)
  Pallas kernels  18.2 us (32%)
  local copies, waits for them, and re-layouts  1.61 us (3%)
  loops' own time  1.49 us (3%)
    all_to_all x2, blocking collectives, exchange(): lax.all_to_all(value, ('slab', 'grp'), split_axis=0, concat_axis=0, tiled...  35.5 us
    pallas_call x1, Pallas kernels, spectrum_of(): pl.pallas_call(functools.partial(spectrum_kernel, sources, groups, kx_own...  14.6 us
    pallas_call x1, Pallas kernels, route_tiles(): pl.pallas_call(functools.partial(route_kernel, sources, groups), in_specs...  2.03 us
    pallas_call x1, Pallas kernels, pack_tiles(): pl.pallas_call(functools.partial(pack_kernel, copies), in_specs=[pl.Block...  1.57 us
    another operation x1, loops' own time, local(): return lax.while_loop(more, again, (most[1], most[0], found))[2]  1.49 us

profile of v1, /device:TPU:1, one launch (start us, length us, event | category | flops | bytes accessed | tf_op | source)
XLA Modules:
  0.0 56.9 jit_solution(18440488666979954785)
XLA Ops:
  0.0 0.0 copy-start
  0.0 0.1 pad_add_fusion.place_ref
  0.1 1.6 %pack_tiles.1 = f32[272,128]{1,0:T(8,128)} custom-call(s32[2]{0:T(128)S(1)} %pad_add_fusion.place_ref, f32[32,64]{1,0:T(8,128)} %bitcast.27, s32[3,32]{1,0:T(4,128)} %centres_ref.1, f32[1,32]{1,0:T(1,128)} %bitcast.28, s32[1,32]{1,0:T(1,128)} %bitcast.29), custom_call_target="tpu_custom_call" | custom-call | tf_op jit(solution)/shard_map/pack_tiles/pallas_call | solution.py:52
  1.6 19.0 %all_to_all.18 = f32[16,1,2176]{2,1,0:T(1,128)S(1)} all-to-all(f32[16,1,2176]{2,1,0:T(1,128)} %bitcast.26), channel_id=1, replica_groups={{0,1,8,9,16,17,24,25,32,33,40,41,48,49,56,57},{2,3,10,11,18,19,26,27,34..., dimensions={0} | all-to-all | bytes 278528 | tf_op jit(solution)/shard_map/all_to_all | solution.py:435
  20.7 2.0 %route_tiles.2 = f32[896,128]{1,0:T(8,128)} custom-call(s32[2]{0:T(128)S(1)} %pad_add_fusion.place_ref, s32[1]{0:T(128)} %constant.16.clone.1.round_ref, f32[272,128]{1,0:T(8,128)S(1)} %bitcast.23), custom_call_target="tpu_custom_call" | custom-call | tf_op jit(solution)/shard_map/route_tiles/pallas_call | solution.py:148
  22.7 0.0 copy-start.1
  22.7 16.5 %all_to_all.19 = f32[16,56,128]{2,1,0:T(8,128)S(1)} all-to-all(f32[16,56,128]{2,1,0:T(8,128)} %bitcast.25), channel_id=1, replica_groups={{0,2,4,6,64,66,68,70,128,130,132,134,192,194,196,198},{1,3,5,7,65,67,69..., dimensions={0} | all-to-all | bytes 917504 | tf_op jit(solution)/shard_map/all_to_all | solution.py:435
  39.2 0.0 copy-done
  39.2 14.6 %spectrum_of_tiles.2 = (f32[2,8,64,256]{3,2,1,0:T(8,128)S(1)}, s32[2]{0:T(128)S(1)}) custom-call(s32[2]{0:T(128)S(1)} %pad_add_fusion.place_ref, f32[896,128]{1,0:T(8,128)S(1)} %bitcast.21, bf16[2,512,512]{2,1,0:T(8,128)(2,1)S(1)} %copy-done), custom_call_target="tpu_custom_call" | custom-call | tf_op jit(solution)/shard_map/spectrum_of_tiles/pallas_call | solution.py:397
  53.8 0.6 %fusion = (s32[1]{0:T(128)}, s32[1]{0:T(128)}) fusion(s32[2]{0:T(128)S(1)} %get-tuple-element.41), kind=kLoop, calls=%fused_computation.1 | loop fusion | bytes 16 | tf_op jit(solution)/shard_map/slice | solution.py:475
  54.4 0.0 copy-done.1
  54.5 1.5 %while.11 = (s32[]{:T(128)}, f32[2,8,64,256]{3,2,1,0:T(8,128)S(1)}, s32[]{:T(128)}, s32[2]{0:T(128)S(1)}, f32[272,128]{1,0:T(8,128)S(1)}, /*index=5*/s32[]{:T(128)}, bf16[2,512,512]{2,1,0:T(8,128)(2,1)S(1)}) while((s32[]{:T(128)}, f32[2,8,64,256]{3,2,1,0:T(8,128)S(1)}, s32[]{:T(128)}, s32[2]{0:T(128)S(1)}, ...), condition=%wide.region_1.0_spmd.clone, body=%wide.region_0.0_spmd.sunk.clone.sunk | while | flops 3 | bytes 1376377 | solution.py:475
  55.9 0.0 copy-start.2
  56.0 1.0 %copy-done.2 = f32[2,8,64,256]{3,2,1,0:T(8,128)} copy-done((f32[2,8,64,256]{3,2,1,0:T(8,128)}, f32[2,8,64,256]{3,2,1,0:T(8,128)S(1)}, u32[]{:S(2)}) %copy-start.2) | copy-done | bytes 1048600
Async XLA Ops:
  0.0 39.2 %copy-start = (bf16[2,512,512]{2,1,0:T(8,128)(2,1)S(1)}, bf16[2,512,512]{2,1,0:T(8,128)(2,1)}, u32[]{:S(2)}) copy-start(bf16[2,512,512]{2,1,0:T(8,128)(2,1)} %constant.17.clone.wave) | copy-start | bytes 3145732
  22.7 31.7 %copy-start.1 = (bf16[2,512,512]{2,1,0:T(8,128)(2,1)S(1)}, bf16[2,512,512]{2,1,0:T(8,128)(2,1)}, u32[]{:S(2)}) copy-start(bf16[2,512,512]{2,1,0:T(8,128)(2,1)} %constant.17.clone..sunk.2) | copy-start | bytes 3145732
  55.9 1.0 %copy-start.2 = (f32[2,8,64,256]{3,2,1,0:T(8,128)}, f32[2,8,64,256]{3,2,1,0:T(8,128)S(1)}, u32[]{:S(2)}) copy-start(f32[2,8,64,256]{3,2,1,0:T(8,128)S(1)} %get-tuple-element.135) | copy-start | bytes 3145732

commit v2 on v1

--- a/solution.py
+++ b/solution.py
@@ -31,7 +31,7 @@
     return high, (value - high.astype(F32)).astype(BF16)
 
 
-def pack_kernel(copies, place_ref, coeffs_ref, centres_ref, exponents_ref, live_ref, out_ref, block):
+def pack_kernel(copies, coeffs_ref, centres_ref, exponents_ref, live_ref, out_ref, block):
     half = coeffs_ref.shape[0] // 2
     block[0:half, 0:TERMS] = coeffs_ref[0:half, :]
     block[0:half, TERMS:] = coeffs_ref[half:, :]
@@ -47,16 +47,13 @@
         out_ref[copy * ROWS : (copy + 1) * ROWS, :] = value
 
 
-def pack_tiles(copies, place, tile_centres, tile_coeffs, tile_exponents, tile_live):
-    vmem = pl.BlockSpec(memory_space=pltpu.VMEM)
+def pack_tiles(copies, tile_centres, tile_coeffs, tile_exponents, tile_live):
     return pl.pallas_call(
         functools.partial(pack_kernel, copies),
-        in_specs=[pl.BlockSpec(memory_space=pltpu.SMEM), vmem, vmem, vmem, vmem],
-        out_specs=vmem,
         out_shape=jax.ShapeDtypeStruct((copies * ROWS, LANES), F32),
         scratch_shapes=[pltpu.VMEM((ROWS, LANES), F32)],
         name="pack_tiles",
-    )(place, tile_coeffs.T, tile_centres, tile_exponents[None, :], tile_live[None, :])
+    )(tile_coeffs.T, tile_centres, tile_exponents[None, :], tile_live[None, :])
 
 
 def route_kernel(sources, groups, place_ref, round_ref, tiles_ref, out_ref, rows_ref, table, rank_ref, count_ref):
@@ -174,30 +171,35 @@
     return found
 
 
-def merge_sources(sources, tiles_ref, bins):
+def merge_sources(sources, tiles_ref, bins, count_ref):
     lane = lax.broadcasted_iota(jnp.int32, (8, LANES), 1)
     first = LANES // 2
     counts = [tiles_ref[pl.ds(52 + k, sources, stride=BLOCK), :] for k in range(3)]
+    scalars = [
+        [jnp.max(count[source : source + 1, :]).astype(jnp.int32) for count in counts]
+        for source in range(sources)
+    ]
+    for source in range(sources):
+        for kind in range(3):
+            count_ref[kind, source] = scalars[source][kind]
     ends = [jnp.int32(0), jnp.int32(0)]
     open_column = [[jnp.zeros((8, LANES), F32)] * (FEAT // 8) for _ in range(2)]
     for source in range(sources):
-        held, upto, start = (
-            jnp.max(count[source : source + 1, :]).astype(jnp.int32) for count in counts
-        )
+        held, upto, start = scalars[source]
         at = source * BLOCK
         pieces = [tiles_ref[at + row : at + row + 8, :] for row in range(0, 32, 8)]
         numbers = tiles_ref[at + 48 : at + 56, :]
         for half, (begin, end) in enumerate(((jnp.int32(0), upto), (start, held))):
             begin, end = jnp.minimum(begin, first), jnp.minimum(end, first)
-            column = ends[half] // LANES
-            offset = ends[half] % LANES
-            shift = (offset - begin + LANES) % LANES
+            column = ends[half] >> 7
+            offset = ends[half] & (LANES - 1)
+            shift = (offset - begin) & (LANES - 1)
             after = ends[half] + (end - begin)
             kept = lane < offset
-            stays = after // LANES == column
+            stays = after >> 7 == column
             lower = (lane >= begin) & (lane < end)
             upper = (lane >= begin + first) & (lane < end + first)
-            other = (shift + first) % LANES
+            other = (shift + first) & (LANES - 1)
             moved = [pltpu.roll(jnp.where(lower, piece, 0.0), shift, 1) for piece in pieces]
             moved += [pltpu.roll(jnp.where(upper, piece, 0.0), other, 1) for piece in pieces]
             moved.append(pltpu.roll(jnp.where(lower, numbers, 0.0), shift, 1))
@@ -209,28 +211,28 @@
             ends[half] = after
     for half in range(2):
         for part in range(FEAT // 8):
-            bins[half, ends[half] // LANES, 8 * part : 8 * part + 8, :] = open_column[half][part]
+            bins[half, ends[half] >> 7, 8 * part : 8 * part + 8, :] = open_column[half][part]
 
     def rest(source, ends):
         at = pl.multiple_of(source * BLOCK, 8)
-        numbers = tiles_ref[pl.ds(at + 48, 8), :]
-        held, upto, start = (jnp.max(numbers[4 + k : 5 + k]).astype(jnp.int32) for k in range(3))
+        held, upto, start = (count_ref[kind, source] for kind in range(3))
 
         def append(ends):
+            numbers = tiles_ref[pl.ds(at + 48, 8), :]
             lines = [tiles_ref[pl.ds(at + 32 + row, 8), :] for row in (0, 8)]
             result = []
             for half, (begin, end) in enumerate(((jnp.int32(0), upto), (start, held))):
                 begin, end = jnp.maximum(begin, first) - first, jnp.maximum(end, first) - first
-                column = ends[half] // LANES
-                offset = ends[half] % LANES
+                column = ends[half] >> 7
+                offset = ends[half] & (LANES - 1)
                 kept = lane < offset
                 moved = []
                 for quarter in range(4):
                     valid = (lane >= begin + 32 * quarter) & (lane < end + 32 * quarter)
-                    shift = (offset - begin - 32 * quarter + 2 * LANES) % LANES
+                    shift = (offset - begin - 32 * quarter) & (LANES - 1)
                     moved += [pltpu.roll(jnp.where(valid, line, 0.0), shift, 1) for line in lines]
                 valid = (lane >= begin + first) & (lane < end + first)
-                shift = (offset - begin - first + 2 * LANES) % LANES
+                shift = (offset - begin - first) & (LANES - 1)
                 moved.append(pltpu.roll(jnp.where(valid, numbers, 0.0), shift, 1))
                 for part, piece in enumerate(moved):
                     rows = slice(8 * part, 8 * part + 8)
@@ -250,7 +252,7 @@
     if later:
         before_ref, *refs = refs
     out_ref, most_ref, bins, total, *refs = refs
-    lhs_0, lhs_1, rhs_0, rhs_1, weights_0, weights_1, turn_ref, stage, sems = refs
+    lhs_0, lhs_1, rhs_0, rhs_1, weights_0, weights_1, turn_ref, count_ref, stage, sems = refs
     rows_own = NY // groups
     rows_half = rows_own // 2
     first_kx = place_ref[0] * kx_own
@@ -267,14 +269,11 @@
     for d in range(1, HALF + 1):
         turn_ref[d - 1] = cosine[d]
         turn_ref[HALF + d - 1] = sine[d]
-    total[...] = jnp.zeros_like(total)
-    lhs_1[...] = jnp.zeros_like(lhs_1)
-    rhs_1[...] = jnp.zeros_like(rhs_1)
+    total[1] = jnp.zeros((size, depth), F32)
     most_ref[0] = jnp.max(tiles_ref[pl.ds(55, sources, stride=BLOCK), :]).astype(jnp.int32)
-    most_ref[1] = jnp.int32(1)
-    ends = merge_sources(sources, tiles_ref, bins)
-    lower = (ends[0] + LANES - 1) // LANES
-    upper = jnp.maximum((ends[1] + LANES - 1) // LANES, 1)
+    ends = merge_sources(sources, tiles_ref, bins, count_ref)
+    lower = (ends[0] + LANES - 1) >> 7
+    upper = jnp.maximum((ends[1] + LANES - 1) >> 7, 1)
 
     def build(index, lhs, rhs, weights_x):
         half = (index >= lower).astype(jnp.int32)
@@ -342,45 +341,48 @@
         half = (index >= lower).astype(jnp.int32)
         total[half] += product(lhs, rhs)
 
+    def multiply_built(index, lhs, rhs):
+        half = (index >= lower).astype(jnp.int32)
+        total[half] = jnp.where(index >= 0, total[half] + product(lhs, rhs), 0.0)
+
     def two_blocks(pair, carry):
-        multiply(2 * pair - 1, lhs_1, rhs_1)
+        multiply_built(2 * pair - 1, lhs_1, rhs_1)
         build(2 * pair, lhs_0, rhs_0, weights_0)
         multiply(2 * pair, lhs_0, rhs_0)
         build(2 * pair + 1, lhs_1, rhs_1, weights_1)
         return carry
 
     blocks = lower + upper
-    lax.fori_loop(0, blocks // 2, two_blocks, 0)
-    @pl.when(blocks % 2 == 0)
+    lax.fori_loop(0, blocks >> 1, two_blocks, 0)
+
+    @pl.when(blocks & 1 == 0)
     def _():
         total[1] += product(lhs_1, rhs_1)
 
-    @pl.when(blocks % 2 == 1)
+    @pl.when(blocks & 1 == 1)
     def _():
-        multiply(blocks - 2, lhs_1, rhs_1)
+        multiply_built(blocks - 2, lhs_1, rhs_1)
         build(blocks - 1, lhs_0, rhs_0, weights_0)
         total[1] += product(lhs_0, rhs_0)
 
-    parts = []
-    for half in range(2):
-        real_high, real_low = split(total[half, 0 : size // 2])
-        imag_high, imag_low = split(total[half, size // 2 :])
-        high = jnp.concatenate([real_high, imag_high], axis=1)
-        low = jnp.concatenate([real_low, imag_low], axis=1)
-        parts.append((high, low))
+    real_high, real_low = split(total[:, 0 : size // 2].reshape(size, depth))
+    imag_high, imag_low = split(total[:, size // 2 :].reshape(size, depth))
+    high = jnp.concatenate([real_high, imag_high], axis=1)
+    low = jnp.concatenate([real_low, imag_low], axis=1)
     for part in range(2):
         if later:
             pltpu.sync_copy(before_ref.at[part], stage.at[part])
         columns = slice(part * depth, (part + 1) * depth)
-        for half, (high, low) in enumerate(parts):
-            found = jnp.dot(high, wave[0, :, columns], preferred_element_type=F32)
-            found = found + jnp.dot(low, wave[0, :, columns], preferred_element_type=F32)
-            found = found + jnp.dot(high, wave[1, :, columns], preferred_element_type=F32)
-            found = found.reshape(kx_own, rows_half, depth)
+        found = jnp.dot(high, wave[0, :, columns], preferred_element_type=F32)
+        found = found + jnp.dot(low, wave[0, :, columns], preferred_element_type=F32)
+        found = found + jnp.dot(high, wave[1, :, columns], preferred_element_type=F32)
+        found = found.reshape(2, kx_own, rows_half, depth)
+        for half in range(2):
             rows = slice(half * rows_half, (half + 1) * rows_half)
+            value = found[half]
             if later:
-                found = found + stage[part, :, rows, :]
-            stage[part, :, rows, :] = found
+                value = value + stage[part, :, rows, :]
+            stage[part, :, rows, :] = value
         pltpu.make_async_copy(stage.at[part], out_ref.at[part], sems.at[part]).start()
     for part in range(2):
         pltpu.make_async_copy(stage.at[part], out_ref.at[part], sems.at[part]).wait()
@@ -400,7 +402,7 @@
         out_specs=[hbm, smem],
         out_shape=[
             jax.ShapeDtypeStruct((2, kx_own, rows_own, depth), F32),
-            jax.ShapeDtypeStruct((2,), jnp.int32),
+            jax.ShapeDtypeStruct((1,), jnp.int32),
         ],
         input_output_aliases={3: 0} if later else {},
         scratch_shapes=[
@@ -413,6 +415,7 @@
             pltpu.VMEM((NPOW * NPOW, 2 * kx_own, LANES), F32),
             pltpu.VMEM((NPOW * NPOW, 2 * kx_own, LANES), F32),
             pltpu.VMEM((2 * HALF, kx_own, LANES), F32),
+            pltpu.SMEM((3, sources), jnp.int32),
             pltpu.VMEM((2, kx_own, rows_own, depth), F32),
             pltpu.SemaphoreType.DMA((2,)),
         ],
@@ -455,7 +458,7 @@
     sharers, chunks = len(share[0]), len(spread[0])
     place = jnp.stack([slab, grp]).astype(jnp.int32)
     wave = jnp.asarray(wave_table(depth))
-    packed = pack_tiles(sharers, place, tile_centres, tile_coeffs, tile_exponents, tile_live)
+    packed = pack_tiles(sharers, tile_centres, tile_coeffs, tile_exponents, tile_live)
     tiles = exchange(packed.reshape(sharers, 1, ROWS * LANES), share).reshape(sharers * ROWS, LANES)
 
     def one_round(index, before=None):
@@ -472,7 +475,7 @@
         index, most, found = state
         return index + 1, most, one_round(index, found)[0]
 
-    return lax.while_loop(more, again, (most[1], most[0], found))[2]
+    return lax.while_loop(more, again, (jnp.int32(1), most[0], found))[2]
 
 
 def solution(mesh):

time: 57.3 us -> 52 us (0.908)
  blocking collectives: 35.5 us -> 0 us
  waiting for transfers between devices: 0 us -> 18.6 us
  starting transfers between devices: 0 us -> 16.9 us
  Pallas kernels: 18.2 us -> 15.5 us
  local copies, waits for them, and re-layouts: 1.61 us -> 0.01 us
  loops' own time: 1.49 us -> 0.63 us
    all_to_all x2 -> x0, blocking collectives: 35.5 us -> none  [exchange(): lax.all_to_all(value, ('slab', 'grp'), split_axis=0, concat_axis=0, tiled...]
    all_to_all x0 -> x2, waiting for transfers between devices: none -> 18.6 us  [exchange(): lax.all_to_all(value, ('slab', 'grp'), split_axis=0, concat_axis=0, tiled...]
    all_to_all x0 -> x2, starting transfers between devices: none -> 16.9 us  [exchange(): lax.all_to_all(value, ('slab', 'grp'), split_axis=0, concat_axis=0, tiled...]
    pallas_call x1, Pallas kernels: 14.6 us -> 11.9 us  [spectrum_of(): pl.pallas_call(functools.partial(spectrum_kernel, sources, groups, kx_own...]
    unnamed x6 -> x4, local copies, waits for them, and re-layouts: 0.97 us -> 0.01 us
    another operation x1, loops' own time: 1.49 us -> 0.63 us  [local(): return lax.while_loop(more, again, (jnp.int32(1), most[0], found))[2]]
    slice x1 -> x0, local copies, waits for them, and re-layouts: 0.63 us -> none  [local(): return lax.while_loop(more, again, (most[1], most[0], found))[2]]
  transfers between devices with their start and end apart: 0 -> 2, of which waited for: 0 -> 2; matrix products, arithmetic and copies ran while one was open for 0% -> 0% of each run, Pallas kernels for 0% -> 0%
where the time goes in v2:
time: 52 us; the launch traced here: 51.7 us
  waiting for transfers between devices  18.6 us (36%)
  starting transfers between devices  16.9 us (32%)
  Pallas kernels  15.5 us (30%)
  loops' own time  0.63 us (1%)
    all_to_all x2, waiting for transfers between devices, exchange(): lax.all_to_all(value, ('slab', 'grp'), split_axis=0, concat_axis=0, tiled...  18.6 us
    all_to_all x2, starting transfers between devices, exchange(): lax.all_to_all(value, ('slab', 'grp'), split_axis=0, concat_axis=0, tiled...  16.9 us
    pallas_call x1, Pallas kernels, spectrum_of(): pl.pallas_call(functools.partial(spectrum_kernel, sources, groups, kx_own...  11.9 us
    pallas_call x1, Pallas kernels, route_tiles(): pl.pallas_call(functools.partial(route_kernel, sources, groups), in_specs...  2.03 us
    pallas_call x1, Pallas kernels, pack_tiles(): pl.pallas_call(functools.partial(pack_kernel, copies), out_shape=jax.Shap...  1.58 us
  transfers between devices with their start and end apart: 2, of which 2 were waited for; matrix products, arithmetic and copies ran while one was open for 0% of the time, Pallas kernels for 0%

profile of v2, /device:TPU:1, one launch (start us, length us, event | category | flops | bytes accessed | tf_op | source)
XLA Modules:
  0.0 51.7 jit_solution(14300177069991743306)
XLA Ops:
  0.0 0.0 copy-start
  0.0 1.6 %pack_tiles.1 = f32[272,128]{1,0:T(8,128)} custom-call(f32[32,64]{1,0:T(8,128)} %bitcast.26, s32[3,32]{1,0:T(4,128)} %centres_ref.1, f32[1,32]{1,0:T(1,128)} %bitcast.27, s32[1,32]{1,0:T(1,128)} %bitcast.28), custom_call_target="tpu_custom_call" | custom-call | tf_op jit(solution)/shard_map/pack_tiles/pallas_call | solution.py:51
  1.6 10.0 %all-to-all-start.1 = ((f32[16,1,2176]{2,1,0:T(1,128)}), f32[16,1,2176]{2,1,0:T(1,128)S(1)}, u32[]{:S(2)}, u32[]{:S(2)}) async-start(f32[16,1,2176]{2,1,0:T(1,128)} %bitcast.25), calls=%async_computation.1 | async-start | bytes 278528 | tf_op jit(solution)/shard_map/all_to_all | solution.py:438
  11.6 0.1 pad_add_fusion.place_ref
  11.6 9.0 %all-to-all-done.1 = f32[16,1,2176]{2,1,0:T(1,128)S(1)} async-done(((f32[16,1,2176]{2,1,0:T(1,128)}), f32[16,1,2176]{2,1,0:T(1,128)S(1)}, u32[]{:S(2)}, u32[]{:S(2)}) %all-to-all-start.1) | async-done | bytes 139296 | tf_op jit(solution)/shard_map/all_to_all | solution.py:438
  20.6 2.0 %route_tiles.2 = f32[896,128]{1,0:T(8,128)} custom-call(s32[2]{0:T(128)S(1)} %pad_add_fusion.place_ref, s32[1]{0:T(128)} %constant.18.clone.1.round_ref, f32[272,128]{1,0:T(8,128)S(1)} %bitcast.22), custom_call_target="tpu_custom_call" | custom-call | tf_op jit(solution)/shard_map/route_tiles/pallas_call | solution.py:145
  22.6 0.0 copy-start.1
  22.6 6.9 %all-to-all-start.2 = ((f32[16,56,128]{2,1,0:T(8,128)}), f32[16,56,128]{2,1,0:T(8,128)S(1)}, u32[]{:S(2)}, u32[]{:S(2)}) async-start(f32[16,56,128]{2,1,0:T(8,128)} %bitcast.24), calls=%async_computation.2 | async-start | bytes 917504 | tf_op jit(solution)/shard_map/all_to_all | solution.py:438
  29.5 9.6 %all-to-all-done.2 = f32[16,56,128]{2,1,0:T(8,128)S(1)} async-done(((f32[16,56,128]{2,1,0:T(8,128)}), f32[16,56,128]{2,1,0:T(8,128)S(1)}, u32[]{:S(2)}, u32[]{:S(2)}) %all-to-all-start.2) | async-done | bytes 458784 | tf_op jit(solution)/shard_map/all_to_all | solution.py:438
  39.2 0.0 copy-done
  39.2 11.9 %spectrum_of_tiles.2 = (f32[2,8,64,256]{3,2,1,0:T(8,128)}, s32[1]{0:T(128)}) custom-call(s32[2]{0:T(128)S(1)} %pad_add_fusion.place_ref, f32[896,128]{1,0:T(8,128)S(1)} %bitcast.20, bf16[2,512,512]{2,1,0:T(8,128)(2,1)S(1)} %copy-done), custom_call_target="tpu_custom_call" | custom-call | tf_op jit(solution)/shard_map/spectrum_of_tiles/pallas_call | solution.py:399
  51.1 0.0 copy-done.1
  51.1 0.6 %while.11 = (s32[]{:T(128)}, f32[2,8,64,256]{3,2,1,0:T(8,128)}, s32[]{:T(128)}, s32[2]{0:T(128)S(1)}, f32[272,128]{1,0:T(8,128)S(1)}, /*index=5*/s32[]{:T(128)}, bf16[2,512,512]{2,1,0:T(8,128)(2,1)S(1)}) while((s32[]{:T(128)}, f32[2,8,64,256]{3,2,1,0:T(8,128)}, s32[]{:T(128)}, s32[2]{0:T(128)S(1)}, f32[272,128]{1,0:T(8,128)S(1)}, ...), condition=%wide.region_1.0_spmd.clone, body=%wide.region_0.0_spmd.sunk.clone.sunk | while | flops 3 | bytes 9765041 | solution.py:478
Async XLA Ops:
  0.0 39.2 %copy-start = (bf16[2,512,512]{2,1,0:T(8,128)(2,1)S(1)}, bf16[2,512,512]{2,1,0:T(8,128)(2,1)}, u32[]{:S(2)}) copy-start(bf16[2,512,512]{2,1,0:T(8,128)(2,1)} %constant.19.clone.wave) | copy-start | bytes 3145732
  1.6 19.0 %all-to-all-start.1 = ((f32[16,1,2176]{2,1,0:T(1,128)}), f32[16,1,2176]{2,1,0:T(1,128)S(1)}, u32[]{:S(2)}, u32[]{:S(2)}) async-start(f32[16,1,2176]{2,1,0:T(1,128)} %bitcast.25), calls=%async_computation.1 | async-start | bytes 278528 | tf_op jit(solution)/shard_map/all_to_all | solution.py:438
  22.6 28.4 %copy-start.1 = (bf16[2,512,512]{2,1,0:T(8,128)(2,1)S(1)}, bf16[2,512,512]{2,1,0:T(8,128)(2,1)}, u32[]{:S(2)}) copy-start(bf16[2,512,512]{2,1,0:T(8,128)(2,1)} %constant.19.clone..sunk.2) | copy-start | bytes 3145732
  22.6 16.5 %all-to-all-start.2 = ((f32[16,56,128]{2,1,0:T(8,128)}), f32[16,56,128]{2,1,0:T(8,128)S(1)}, u32[]{:S(2)}, u32[]{:S(2)}) async-start(f32[16,56,128]{2,1,0:T(8,128)} %bitcast.24), calls=%async_computation.2 | async-start | bytes 917504 | tf_op jit(solution)/shard_map/all_to_all | solution.py:438

commit v3 on v2

--- a/solution.py
+++ b/solution.py
@@ -56,7 +56,9 @@
     )(tile_coeffs.T, tile_centres, tile_exponents[None, :], tile_live[None, :])
 
 
-def route_kernel(sources, groups, place_ref, round_ref, tiles_ref, out_ref, rows_ref, table, rank_ref, count_ref):
+def route_kernel(
+    sources, groups, round_ref, tiles_ref, out_ref, rows_ref, table, rank_ref, count_ref, blocks, sem
+):
     per_row = 16
     side = sources * per_row
     total = 2 * side
@@ -109,7 +111,7 @@
             index += 1
         count_ref[kind] = jnp.broadcast_to(count, (groups, LANES))
     base = (round_ref[0] * SLOTS).astype(F32)
-    core = place_ref[1] % 2
+    core = lax.axis_index("grp") % 2
     high, low = split(table[...])
     both = jnp.concatenate([high, low], axis=0)
     depth = table.shape[0]
@@ -117,6 +119,7 @@
     slot = lax.broadcasted_iota(jnp.int32, (LANES, total), 0).astype(F32)
     lane = lax.broadcasted_iota(jnp.int32, (32, LANES), 1)
     rows_y = groups // 2
+    copies = []
     for target in range(rows_y):
         own_row = pl.ds(2 * target + core, 1)
         ranks = rank_ref[own_row, :] - base
@@ -134,31 +137,36 @@
         numbers = jnp.concatenate(
             [got[TERMS : TERMS + 4], ends[2], ends[1], ends[0], jnp.full((1, LANES), most, F32)], axis=0
         )
-        for copy in range(out_ref.shape[0] // (BLOCK * rows_y)):
-            at = (copy * rows_y + target) * BLOCK
-            out_ref[at : at + 32, :] = first
-            out_ref[at + 32 : at + 48, :] = extra
-            out_ref[at + 48 : at + 56, :] = numbers
-
-
-def route_tiles(sources, targets, groups, place, round_index, tiles):
+        blocks[target, 0:32, :] = first
+        blocks[target, 32:48, :] = extra
+        blocks[target, 48:56, :] = numbers
+        for copy in range(out_ref.shape[0] // rows_y):
+            at = copy * rows_y + target
+            copies.append(pltpu.make_async_copy(blocks.at[target], out_ref.at[at], sem.at[at]))
+            copies[-1].start()
+    for copy in copies:
+        copy.wait()
+
+
+def route_tiles(sources, targets, groups, round_index, tiles):
     return pl.pallas_call(
         functools.partial(route_kernel, sources, groups),
         in_specs=[
             pl.BlockSpec(memory_space=pltpu.SMEM),
-            pl.BlockSpec(memory_space=pltpu.SMEM),
             pl.BlockSpec(memory_space=pltpu.VMEM),
         ],
-        out_specs=pl.BlockSpec(memory_space=pltpu.VMEM),
-        out_shape=jax.ShapeDtypeStruct((targets * BLOCK, LANES), F32),
+        out_specs=pl.BlockSpec(memory_space=pltpu.HBM),
+        out_shape=jax.ShapeDtypeStruct((targets, BLOCK, LANES), F32),
         scratch_shapes=[
             pltpu.VMEM((sources * 16, LANES), F32),
             pltpu.VMEM((80, sources * 32), F32),
             pltpu.VMEM((groups, sources * 32), F32),
             pltpu.VMEM((3, groups, LANES), F32),
+            pltpu.VMEM((groups // 2, BLOCK, LANES), F32),
+            pltpu.SemaphoreType.DMA((targets,)),
         ],
         name="route_tiles",
-    )(place, round_index, tiles)
+    )(round_index, tiles)
 
 
 def powers_of(distance, rate):
@@ -247,16 +255,17 @@
 
 
 def spectrum_kernel(
-    sources, groups, kx_own, depth, later, place_ref, tiles_ref, wave, *refs
+    sources, groups, kx_own, depth, later, tiles_ref, wave, *refs
 ):
     if later:
         before_ref, *refs = refs
     out_ref, most_ref, bins, total, *refs = refs
-    lhs_0, lhs_1, rhs_0, rhs_1, weights_0, weights_1, turn_ref, count_ref, stage, sems = refs
+    lhs, rhs, weights, turn_ref, count_ref, stage, sems = refs
+    lhs, rhs, weights = ([ref.at[slot] for slot in range(4)] for ref in (lhs, rhs, weights))
     rows_own = NY // groups
     rows_half = rows_own // 2
-    first_kx = place_ref[0] * kx_own
-    first_y = place_ref[1] * rows_own
+    first_kx = lax.axis_index("slab") * kx_own
+    first_y = lax.axis_index("grp") * rows_own
     size = 2 * kx_own * rows_half
     scale = 1.0 / math.sqrt(NX * depth)
     kx = first_kx + lax.broadcasted_iota(jnp.int32, (kx_own, LANES), 0)
@@ -269,11 +278,11 @@
     for d in range(1, HALF + 1):
         turn_ref[d - 1] = cosine[d]
         turn_ref[HALF + d - 1] = sine[d]
-    total[1] = jnp.zeros((size, depth), F32)
+    total[...] = jnp.zeros_like(total)
     most_ref[0] = jnp.max(tiles_ref[pl.ds(55, sources, stride=BLOCK), :]).astype(jnp.int32)
     ends = merge_sources(sources, tiles_ref, bins, count_ref)
     lower = (ends[0] + LANES - 1) >> 7
-    upper = jnp.maximum((ends[1] + LANES - 1) >> 7, 1)
+    upper = (ends[1] + LANES - 1) >> 7
 
     def build(index, lhs, rhs, weights_x):
         half = (index >= lower).astype(jnp.int32)
@@ -337,49 +346,49 @@
         right = jnp.concatenate([rhs[k] for k in (*highs, *highs, *lows)], axis=1)
         return lax.dot_general(left, right, NT, preferred_element_type=F32)
 
-    def multiply(index, lhs, rhs):
+    def multiply(index, slot):
         half = (index >= lower).astype(jnp.int32)
-        total[half] += product(lhs, rhs)
-
-    def multiply_built(index, lhs, rhs):
-        half = (index >= lower).astype(jnp.int32)
-        total[half] = jnp.where(index >= 0, total[half] + product(lhs, rhs), 0.0)
-
-    def two_blocks(pair, carry):
-        multiply_built(2 * pair - 1, lhs_1, rhs_1)
-        build(2 * pair, lhs_0, rhs_0, weights_0)
-        multiply(2 * pair, lhs_0, rhs_0)
-        build(2 * pair + 1, lhs_1, rhs_1, weights_1)
+        total[half] += product(lhs[slot], rhs[slot])
+
+    def four_blocks(four, carry):
+        half = (4 * four - 1 >= lower).astype(jnp.int32)
+        total[half] += jnp.where(four > 0, product(lhs[3], rhs[3]), 0.0)
+        for slot in range(4):
+            build(4 * four + slot, lhs[slot], rhs[slot], weights[slot])
+            if slot < 3:
+                multiply(4 * four + slot, slot)
         return carry
 
+    def one_block(index, carry):
+        build(index, lhs[0], rhs[0], weights[0])
+        multiply(index, 0)
+        return carry
+
     blocks = lower + upper
-    lax.fori_loop(0, blocks >> 1, two_blocks, 0)
-
-    @pl.when(blocks & 1 == 0)
-    def _():
-        total[1] += product(lhs_1, rhs_1)
-
-    @pl.when(blocks & 1 == 1)
-    def _():
-        multiply_built(blocks - 2, lhs_1, rhs_1)
-        build(blocks - 1, lhs_0, rhs_0, weights_0)
-        total[1] += product(lhs_0, rhs_0)
-
+    built = jnp.int32(0)
+    if not later:
+        built = (blocks >> 2) * 4
+        lax.fori_loop(0, blocks >> 2, four_blocks, 0)
+
+        @pl.when(built > 0)
+        def _():
+            multiply(built - 1, 3)
+
+    lax.fori_loop(built, blocks, one_block, 0)
     real_high, real_low = split(total[:, 0 : size // 2].reshape(size, depth))
     imag_high, imag_low = split(total[:, size // 2 :].reshape(size, depth))
-    high = jnp.concatenate([real_high, imag_high], axis=1)
-    low = jnp.concatenate([real_low, imag_low], axis=1)
+    spectra = jnp.concatenate(
+        [real_high, imag_high, real_low, imag_low, real_high, imag_high], axis=1
+    )
+    waves = jnp.concatenate([wave[0], wave[0], wave[1]], axis=0)
+    found = jnp.dot(spectra, waves, preferred_element_type=F32)
+    found = found.reshape(2, kx_own, rows_half, 2 * depth)
+    if later:
+        pltpu.sync_copy(before_ref, stage)
     for part in range(2):
-        if later:
-            pltpu.sync_copy(before_ref.at[part], stage.at[part])
-        columns = slice(part * depth, (part + 1) * depth)
-        found = jnp.dot(high, wave[0, :, columns], preferred_element_type=F32)
-        found = found + jnp.dot(low, wave[0, :, columns], preferred_element_type=F32)
-        found = found + jnp.dot(high, wave[1, :, columns], preferred_element_type=F32)
-        found = found.reshape(2, kx_own, rows_half, depth)
         for half in range(2):
             rows = slice(half * rows_half, (half + 1) * rows_half)
-            value = found[half]
+            value = found[half, :, :, part * depth : (part + 1) * depth]
             if later:
                 value = value + stage[part, :, rows, :]
             stage[part, :, rows, :] = value
@@ -388,7 +397,7 @@
         pltpu.make_async_copy(stage.at[part], out_ref.at[part], sems.at[part]).wait()
 
 
-def spectrum_of(sources, groups, kx_own, depth, place, tiles, wave, before=None):
+def spectrum_of(sources, groups, kx_own, depth, tiles, wave, before=None):
     rows_own = NY // groups
     size = kx_own * rows_own
     columns = sources * SLOTS // LANES + 2
@@ -398,22 +407,19 @@
     later = before is not None
     return pl.pallas_call(
         functools.partial(spectrum_kernel, sources, groups, kx_own, depth, later),
-        in_specs=[smem, vmem, vmem] + [hbm] * later,
+        in_specs=[vmem, vmem] + [hbm] * later,
         out_specs=[hbm, smem],
         out_shape=[
             jax.ShapeDtypeStruct((2, kx_own, rows_own, depth), F32),
             jax.ShapeDtypeStruct((1,), jnp.int32),
         ],
-        input_output_aliases={3: 0} if later else {},
+        input_output_aliases={2: 0} if later else {},
         scratch_shapes=[
             pltpu.VMEM((2, columns, FEAT, LANES), F32),
             pltpu.VMEM((2, size, depth), F32),
-            pltpu.VMEM((2 * NPOW, size, LANES), BF16),
-            pltpu.VMEM((2 * NPOW, size, LANES), BF16),
-            pltpu.VMEM((2 * NPOW, depth, LANES), BF16),
-            pltpu.VMEM((2 * NPOW, depth, LANES), BF16),
-            pltpu.VMEM((NPOW * NPOW, 2 * kx_own, LANES), F32),
-            pltpu.VMEM((NPOW * NPOW, 2 * kx_own, LANES), F32),
+            pltpu.VMEM((4, 2 * NPOW, size, LANES), BF16),
+            pltpu.VMEM((4, 2 * NPOW, depth, LANES), BF16),
+            pltpu.VMEM((4, NPOW * NPOW, 2 * kx_own, LANES), F32),
             pltpu.VMEM((2 * HALF, kx_own, LANES), F32),
             pltpu.SMEM((3, sources), jnp.int32),
             pltpu.VMEM((2, kx_own, rows_own, depth), F32),
@@ -421,7 +427,7 @@
         ],
         compiler_params=pltpu.CompilerParams(vmem_limit_bytes=40 * 2**20),
         name="spectrum_of_tiles",
-    )(place, tiles, wave, *([before] if later else []))
+    )(tiles, wave, *([before] if later else []))
 
 
 def wave_table(depth):
@@ -443,7 +449,6 @@
 def local(tile_centres, tile_coeffs, tile_exponents, tile_live):
     slab_count = lax.axis_size("slab")
     grp_count = lax.axis_size("grp")
-    slab, grp = lax.axis_index("slab"), lax.axis_index("grp")
     depth = CZ * slab_count
     kx_own = NX // 2 // slab_count
     count_z = slab_count // COUNT_X
@@ -456,15 +461,14 @@
     share = [[device(x, z, y, c) for z in zs for c in cores] for x in xs for y in ys]
     spread = [[device(x, z, y, c) for x in xs for y in ys] for z in zs for c in cores]
     sharers, chunks = len(share[0]), len(spread[0])
-    place = jnp.stack([slab, grp]).astype(jnp.int32)
     wave = jnp.asarray(wave_table(depth))
     packed = pack_tiles(sharers, tile_centres, tile_coeffs, tile_exponents, tile_live)
     tiles = exchange(packed.reshape(sharers, 1, ROWS * LANES), share).reshape(sharers * ROWS, LANES)
 
     def one_round(index, before=None):
-        routed = route_tiles(sharers, chunks, grp_count, place, index.reshape(1), tiles)
-        routed = exchange(routed.reshape(chunks, BLOCK, LANES), spread).reshape(chunks * BLOCK, LANES)
-        return spectrum_of(chunks, grp_count, kx_own, depth, place, routed, wave, before)
+        routed = route_tiles(sharers, chunks, grp_count, index.reshape(1), tiles)
+        routed = exchange(routed, spread).reshape(chunks * BLOCK, LANES)
+        return spectrum_of(chunks, grp_count, kx_own, depth, routed, wave, before)
 
     found, most = one_round(jnp.int32(0))
 

time: 52 us -> 50.8 us (0.977)
  blocking collectives: 0 us -> 19 us
  starting transfers between devices: 16.9 us -> 6.9 us
  waiting for transfers between devices: 18.6 us -> 9.63 us
  Pallas kernels: 15.5 us -> 14.3 us
    all_to_all x0 -> x1, blocking collectives: none -> 19 us  [exchange(): lax.all_to_all(value, ('slab', 'grp'), split_axis=0, concat_axis=0, tiled...]
    all_to_all x2 -> x1, starting transfers between devices: 16.9 us -> 6.9 us  [exchange(): lax.all_to_all(value, ('slab', 'grp'), split_axis=0, concat_axis=0, tiled...]
    all_to_all x2 -> x1, waiting for transfers between devices: 18.6 us -> 9.63 us  [exchange(): lax.all_to_all(value, ('slab', 'grp'), split_axis=0, concat_axis=0, tiled...]
    pallas_call x1, Pallas kernels: 11.9 us -> 11.2 us  [spectrum_of(): pl.pallas_call(functools.partial(spectrum_kernel, sources, groups, kx_own...]
  transfers between devices with their start and end apart: 2 -> 1, of which waited for: 2 -> 1; matrix products, arithmetic and copies ran while one was open for 0% -> 0% of each run, Pallas kernels for 0% -> 0%
where the time goes in v3:
time: 50.8 us; the launch traced here: 50.5 us
  blocking collectives  19 us (37%)
  Pallas kernels  14.3 us (28%)
  waiting for transfers between devices  9.63 us (19%)
  starting transfers between devices  6.9 us (14%)
  loops' own time  0.57 us (1%)
    all_to_all x1, blocking collectives, exchange(): lax.all_to_all(value, ('slab', 'grp'), split_axis=0, concat_axis=0, tiled...  19 us
    pallas_call x1, Pallas kernels, spectrum_of(): pl.pallas_call(functools.partial(spectrum_kernel, sources, groups, kx_own...  11.2 us
    all_to_all x1, waiting for transfers between devices, exchange(): lax.all_to_all(value, ('slab', 'grp'), split_axis=0, concat_axis=0, tiled...  9.63 us
    all_to_all x1, starting transfers between devices, exchange(): lax.all_to_all(value, ('slab', 'grp'), split_axis=0, concat_axis=0, tiled...  6.9 us
    pallas_call x1, Pallas kernels, pack_tiles(): pl.pallas_call(functools.partial(pack_kernel, copies), out_shape=jax.Shap...  1.58 us
    pallas_call x1, Pallas kernels, route_tiles(): pl.pallas_call(functools.partial(route_kernel, sources, groups), in_specs...  1.51 us
  transfers between devices with their start and end apart: 1, of which 1 were waited for; matrix products, arithmetic and copies ran while one was open for 0% of the time, Pallas kernels for 0%

profile of v3, /device:TPU:1, one launch (start us, length us, event | category | flops | bytes accessed | tf_op | source)
XLA Modules:
  0.0 50.5 jit_solution(11585126579581210796)
XLA Ops:
  0.0 0.0 copy-start
  0.0 1.6 %pack_tiles.1 = f32[272,128]{1,0:T(8,128)} custom-call(f32[32,64]{1,0:T(8,128)} %bitcast.18, s32[3,32]{1,0:T(4,128)} %centres_ref.1, f32[1,32]{1,0:T(1,128)} %bitcast.19, s32[1,32]{1,0:T(1,128)} %bitcast.20), custom_call_target="tpu_custom_call" | custom-call | tf_op jit(solution)/shard_map/pack_tiles/pallas_call | solution.py:51
  1.6 19.0 %all_to_all.18 = f32[16,1,2176]{2,1,0:T(1,128)S(1)} all-to-all(f32[16,1,2176]{2,1,0:T(1,128)} %bitcast.17), channel_id=1, replica_groups={{0,1,8,9,16,17,24,25,32,33,40,41,48,49,56,57},{2,3,10,11,18,19,26,27,34..., dimensions={0} | all-to-all | bytes 278528 | tf_op jit(solution)/shard_map/all_to_all | solution.py:444
  20.6 1.5 %route_tiles.2 = f32[16,56,128]{2,1,0:T(8,128)} custom-call(s32[1]{0:T(128)} %constant.5.clone.1.round_ref, f32[272,128]{1,0:T(8,128)S(1)} %bitcast.15), custom_call_target="tpu_custom_call" | custom-call | tf_op jit(solution)/shard_map/route_tiles/pallas_call | solution.py:152
  22.1 0.0 copy-start.1
  22.1 6.9 %all-to-all-start.2 = ((f32[16,56,128]{2,1,0:T(8,128)}), f32[16,56,128]{2,1,0:T(8,128)S(1)}, u32[]{:S(2)}, u32[]{:S(2)}) async-start(f32[16,56,128]{2,1,0:T(8,128)} %route_tiles.2), calls=%async_computation.2 | async-start | bytes 917504 | tf_op jit(solution)/shard_map/all_to_all | solution.py:444
  29.1 9.6 %all-to-all-done.2 = f32[16,56,128]{2,1,0:T(8,128)S(1)} async-done(((f32[16,56,128]{2,1,0:T(8,128)}), f32[16,56,128]{2,1,0:T(8,128)S(1)}, u32[]{:S(2)}, u32[]{:S(2)}) %all-to-all-start.2) | async-done | bytes 458784 | tf_op jit(solution)/shard_map/all_to_all | solution.py:444
  38.7 0.0 copy-done
  38.7 11.2 %spectrum_of_tiles.2 = (f32[2,8,64,256]{3,2,1,0:T(8,128)}, s32[1]{0:T(128)}) custom-call(f32[896,128]{1,0:T(8,128)S(1)} %bitcast.14, bf16[2,512,512]{2,1,0:T(8,128)(2,1)S(1)} %copy-done), custom_call_target="tpu_custom_call" | custom-call | tf_op jit(solution)/shard_map/spectrum_of_tiles/pallas_call | solution.py:408
  49.9 0.0 copy-done.1
  49.9 0.6 %while.11 = (s32[]{:T(128)}, f32[2,8,64,256]{3,2,1,0:T(8,128)}, s32[]{:T(128)}, f32[272,128]{1,0:T(8,128)S(1)}, s32[]{:T(128)}, /*index=5*/bf16[2,512,512]{2,1,0:T(8,128)(2,1)S(1)}) while((s32[]{:T(128)}, f32[2,8,64,256]{3,2,1,0:T(8,128)}, s32[]{:T(128)}, f32[272,128]{1,0:T(8,128)S(1)}, s32[]{:T(128)}, ...), condition=%wide.region_1.0_spmd.clone, body=%wide.region_0.0_spmd.sunk.clone.sunk | while | flops 3 | bytes 9765033 | solution.py:482
Async XLA Ops:
  0.0 38.7 %copy-start = (bf16[2,512,512]{2,1,0:T(8,128)(2,1)S(1)}, bf16[2,512,512]{2,1,0:T(8,128)(2,1)}, u32[]{:S(2)}) copy-start(bf16[2,512,512]{2,1,0:T(8,128)(2,1)} %constant.10.clone.wave) | copy-start | bytes 3145732
  22.1 27.8 %copy-start.1 = (bf16[2,512,512]{2,1,0:T(8,128)(2,1)S(1)}, bf16[2,512,512]{2,1,0:T(8,128)(2,1)}, u32[]{:S(2)}) copy-start(bf16[2,512,512]{2,1,0:T(8,128)(2,1)} %constant.10.clone..sunk.2) | copy-start | bytes 3145732
  22.1 16.5 %all-to-all-start.2 = ((f32[16,56,128]{2,1,0:T(8,128)}), f32[16,56,128]{2,1,0:T(8,128)S(1)}, u32[]{:S(2)}, u32[]{:S(2)}) async-start(f32[16,56,128]{2,1,0:T(8,128)} %route_tiles.2), calls=%async_computation.2 | async-start | bytes 917504 | tf_op jit(solution)/shard_map/all_to_all | solution.py:444

commit v4 on v3

--- a/solution.py
+++ b/solution.py
@@ -260,7 +260,7 @@
     if later:
         before_ref, *refs = refs
     out_ref, most_ref, bins, total, *refs = refs
-    lhs, rhs, weights, turn_ref, count_ref, stage, sems = refs
+    lhs, rhs, weights, turn_ref, count_ref, planes_ref, stage, sems = refs
     lhs, rhs, weights = ([ref.at[slot] for slot in range(4)] for ref in (lhs, rhs, weights))
     rows_own = NY // groups
     rows_half = rows_own // 2
@@ -279,6 +279,8 @@
         turn_ref[d - 1] = cosine[d]
         turn_ref[HALF + d - 1] = sine[d]
     total[...] = jnp.zeros_like(total)
+    place = lax.broadcasted_iota(jnp.int32, (depth, LANES), 0)
+    planes_ref[...] = jnp.where(place < depth // 2, 2 * place, 2 * place + 1 - depth)
     most_ref[0] = jnp.max(tiles_ref[pl.ds(55, sources, stride=BLOCK), :]).astype(jnp.int32)
     ends = merge_sources(sources, tiles_ref, bins, count_ref)
     lower = (ends[0] + LANES - 1) >> 7
@@ -332,8 +334,7 @@
                 lhs[third, y_rows, :] = high
                 lhs[NPOW + third, y_rows, :] = low
         shift_z = centre_z - depth // 2
-        z_cells = lax.broadcasted_iota(jnp.int32, (depth, LANES), 0)
-        off_z = ((z_cells - shift_z) & (depth - 1)).astype(F32) - float(depth // 2)
+        off_z = ((planes_ref[...] - shift_z) & (depth - 1)).astype(F32) - float(depth // 2)
         along_z = powers_of(off_z, rate)
         for third in range(NPOW):
             high, low = split(along_z[third])
@@ -377,21 +378,29 @@
     lax.fori_loop(built, blocks, one_block, 0)
     real_high, real_low = split(total[:, 0 : size // 2].reshape(size, depth))
     imag_high, imag_low = split(total[:, size // 2 :].reshape(size, depth))
-    spectra = jnp.concatenate(
-        [real_high, imag_high, real_low, imag_low, real_high, imag_high], axis=1
-    )
-    waves = jnp.concatenate([wave[0], wave[0], wave[1]], axis=0)
-    found = jnp.dot(spectra, waves, preferred_element_type=F32)
-    found = found.reshape(2, kx_own, rows_half, 2 * depth)
+    sums = []
+    for parity in range(2):
+        planes = slice(parity * (depth // 2), (parity + 1) * (depth // 2))
+        high = [real_high[:, planes], imag_high[:, planes]]
+        low = [real_low[:, planes], imag_low[:, planes]]
+        spectra = jnp.concatenate([*high, *low, *high], axis=1)
+        waves = jnp.concatenate([wave[0, parity], wave[0, parity], wave[1, parity]], axis=0)
+        sums.append(jnp.dot(spectra, waves, preferred_element_type=F32))
+    found = [sums[0] + sums[1], sums[0] - sums[1]]
     if later:
         pltpu.sync_copy(before_ref, stage)
     for part in range(2):
         for half in range(2):
             rows = slice(half * rows_half, (half + 1) * rows_half)
-            value = found[half, :, :, part * depth : (part + 1) * depth]
-            if later:
-                value = value + stage[part, :, rows, :]
-            stage[part, :, rows, :] = value
+            for upper_half in range(2):
+                columns = slice(upper_half * (depth // 2), (upper_half + 1) * (depth // 2))
+                value = found[upper_half][
+                    half * (size // 2) : (half + 1) * (size // 2),
+                    part * (depth // 2) : (part + 1) * (depth // 2),
+                ].reshape(kx_own, rows_half, depth // 2)
+                if later:
+                    value = value + stage[part, :, rows, columns]
+                stage[part, :, rows, columns] = value
         pltpu.make_async_copy(stage.at[part], out_ref.at[part], sems.at[part]).start()
     for part in range(2):
         pltpu.make_async_copy(stage.at[part], out_ref.at[part], sems.at[part]).wait()
@@ -422,6 +431,7 @@
             pltpu.VMEM((4, NPOW * NPOW, 2 * kx_own, LANES), F32),
             pltpu.VMEM((2 * HALF, kx_own, LANES), F32),
             pltpu.SMEM((3, sources), jnp.int32),
+            pltpu.VMEM((depth, LANES), jnp.int32),
             pltpu.VMEM((2, kx_own, rows_own, depth), F32),
             pltpu.SemaphoreType.DMA((2,)),
         ],
@@ -432,9 +442,13 @@
 
 def wave_table(depth):
     cells = np.arange(depth)
-    angle = 2.0 * np.pi * (cells[:, None] * cells[None, :] % depth) / depth
+    angle = 2.0 * np.pi * (cells[:, None] * cells[None, : depth // 2] % depth) / depth
     cosine, sine = np.cos(angle), np.sin(angle)
-    table = np.block([[cosine, -sine], [sine, cosine]]).astype(np.float32)
+    tables = []
+    for parity in range(2):
+        c, s = cosine[parity::2], sine[parity::2]
+        tables.append(np.block([[c, -s], [s, c]]))
+    table = np.stack(tables).astype(np.float32)
     high = table.astype(jnp.bfloat16)
     low = (table - high.astype(np.float32)).astype(jnp.bfloat16)
     return np.stack([high, low])

time: 50.8 us -> 50.6 us (level)
  Pallas kernels: 14.3 us -> 13 us
  local copies, waits for them, and re-layouts: 0.01 us -> 0.98 us
    pallas_call x1, Pallas kernels: 11.2 us -> 10 us  [spectrum_of(): pl.pallas_call(functools.partial(spectrum_kernel, sources, groups, kx_own...]
    unnamed x4 -> x6, local copies, waits for them, and re-layouts: 0.01 us -> 0.98 us
where the time goes in v4:
time: 50.6 us; the launch traced here: 50.2 us
  blocking collectives  19 us (38%)
  Pallas kernels  13 us (26%)
  waiting for transfers between devices  9.61 us (19%)
  starting transfers between devices  6.9 us (14%)
  local copies, waits for them, and re-layouts  0.98 us (2%)
  loops' own time  0.63 us (1%)
    all_to_all x1, blocking collectives, exchange(): lax.all_to_all(value, ('slab', 'grp'), split_axis=0, concat_axis=0, tiled...  19 us
    pallas_call x1, Pallas kernels, spectrum_of(): pl.pallas_call(functools.partial(spectrum_kernel, sources, groups, kx_own...  10 us
    all_to_all x1, waiting for transfers between devices, exchange(): lax.all_to_all(value, ('slab', 'grp'), split_axis=0, concat_axis=0, tiled...  9.61 us
    all_to_all x1, starting transfers between devices, exchange(): lax.all_to_all(value, ('slab', 'grp'), split_axis=0, concat_axis=0, tiled...  6.9 us
    pallas_call x1, Pallas kernels, route_tiles(): pl.pallas_call(functools.partial(route_kernel, sources, groups), in_specs...  1.51 us
    pallas_call x1, Pallas kernels, pack_tiles(): pl.pallas_call(functools.partial(pack_kernel, copies), out_shape=jax.Shap...  1.49 us
  transfers between devices with their start and end apart: 1, of which 1 were waited for; matrix products, arithmetic and copies ran while one was open for 0% of the time, Pallas kernels for 0%

profile of v4, /device:TPU:1, one launch (start us, length us, event | category | flops | bytes accessed | tf_op | source)
XLA Modules:
  0.0 50.2 jit_solution(5683285444938258270)
XLA Ops:
  0.0 1.5 %pack_tiles.1 = f32[272,128]{1,0:T(8,128)} custom-call(f32[32,64]{1,0:T(8,128)} %bitcast.18, s32[3,32]{1,0:T(4,128)} %centres_ref.1, f32[1,32]{1,0:T(1,128)} %bitcast.19, s32[1,32]{1,0:T(1,128)} %bitcast.20), custom_call_target="tpu_custom_call" | custom-call | tf_op jit(solution)/shard_map/pack_tiles/pallas_call | solution.py:51
  1.5 19.0 %all_to_all.18 = f32[16,1,2176]{2,1,0:T(1,128)S(1)} all-to-all(f32[16,1,2176]{2,1,0:T(1,128)} %bitcast.17), channel_id=1, replica_groups={{0,1,8,9,16,17,24,25,32,33,40,41,48,49,56,57},{2,3,10,11,18,19,26,27,34..., dimensions={0} | all-to-all | bytes 278528 | tf_op jit(solution)/shard_map/all_to_all | solution.py:458
  20.5 1.5 %route_tiles.2 = f32[16,56,128]{2,1,0:T(8,128)} custom-call(s32[1]{0:T(128)} %constant.5.clone.1.round_ref, f32[272,128]{1,0:T(8,128)S(1)} %bitcast.15), custom_call_target="tpu_custom_call" | custom-call | tf_op jit(solution)/shard_map/route_tiles/pallas_call | solution.py:152
  22.0 0.0 copy-start
  22.1 6.9 %all-to-all-start.2 = ((f32[16,56,128]{2,1,0:T(8,128)}), f32[16,56,128]{2,1,0:T(8,128)S(1)}, u32[]{:S(2)}, u32[]{:S(2)}) async-start(f32[16,56,128]{2,1,0:T(8,128)} %route_tiles.2), calls=%async_computation.2 | async-start | bytes 917504 | tf_op jit(solution)/shard_map/all_to_all | solution.py:458
  29.0 0.0 copy-start.2
  29.0 9.6 %all-to-all-done.2 = f32[16,56,128]{2,1,0:T(8,128)S(1)} async-done(((f32[16,56,128]{2,1,0:T(8,128)}), f32[16,56,128]{2,1,0:T(8,128)S(1)}, u32[]{:S(2)}, u32[]{:S(2)}) %all-to-all-start.2) | async-done | bytes 458784 | tf_op jit(solution)/shard_map/all_to_all | solution.py:458
  38.6 0.0 copy-done
  38.6 10.0 %spectrum_of_tiles.2 = (f32[2,8,64,256]{3,2,1,0:T(8,128)S(1)}, s32[1]{0:T(128)}) custom-call(f32[896,128]{1,0:T(8,128)S(1)} %bitcast.14, bf16[2,2,256,256]{3,2,1,0:T(8,128)(2,1)S(1)} %copy-done), custom_call_target="tpu_custom_call" | custom-call | tf_op jit(solution)/shard_map/spectrum_of_tiles/pallas_call | solution.py:417
  48.6 0.0 copy-done.2
  48.6 0.6 %while.11 = (s32[]{:T(128)}, f32[2,8,64,256]{3,2,1,0:T(8,128)S(1)}, s32[]{:T(128)}, f32[272,128]{1,0:T(8,128)S(1)}, s32[]{:T(128)}, /*index=5*/bf16[2,2,256,256]{3,2,1,0:T(8,128)(2,1)S(1)}) while((s32[]{:T(128)}, f32[2,8,64,256]{3,2,1,0:T(8,128)S(1)}, s32[]{:T(128)}, f32[272,128]{1,0:T(8,128)S(1)}, s32[]{:T(128)}, ...), condition=%wide.region_1.0_spmd.clone, body=%wide.region_0.0_spmd.sunk.clone.sunk | while | flops 3 | bytes 1376369 | solution.py:496
  49.3 0.0 copy-start.1
  49.3 1.0 %copy-done.1 = f32[2,8,64,256]{3,2,1,0:T(8,128)} copy-done((f32[2,8,64,256]{3,2,1,0:T(8,128)}, f32[2,8,64,256]{3,2,1,0:T(8,128)S(1)}, u32[]{:S(2)}) %copy-start.1) | copy-done | bytes 1048600
Async XLA Ops:
  22.0 16.5 %copy-start = (bf16[2,2,256,256]{3,2,1,0:T(8,128)(2,1)S(1)}, bf16[2,2,256,256]{3,2,1,0:T(8,128)(2,1)}, u32[]{:S(2)}) copy-start(bf16[2,2,256,256]{3,2,1,0:T(8,128)(2,1)} %constant.10.clone.wave) | copy-start | bytes 1572868
  22.1 16.5 %all-to-all-start.2 = ((f32[16,56,128]{2,1,0:T(8,128)}), f32[16,56,128]{2,1,0:T(8,128)S(1)}, u32[]{:S(2)}, u32[]{:S(2)}) async-start(f32[16,56,128]{2,1,0:T(8,128)} %route_tiles.2), calls=%async_computation.2 | async-start | bytes 917504 | tf_op jit(solution)/shard_map/all_to_all | solution.py:458
  29.0 19.7 %copy-start.2 = (bf16[2,2,256,256]{3,2,1,0:T(8,128)(2,1)S(1)}, bf16[2,2,256,256]{3,2,1,0:T(8,128)(2,1)}, u32[]{:S(2)}) copy-start(bf16[2,2,256,256]{3,2,1,0:T(8,128)(2,1)} %constant.10.clone..sunk.2) | copy-start | bytes 1572868
  49.3 1.0 %copy-start.1 = (f32[2,8,64,256]{3,2,1,0:T(8,128)}, f32[2,8,64,256]{3,2,1,0:T(8,128)S(1)}, u32[]{:S(2)}) copy-start(f32[2,8,64,256]{3,2,1,0:T(8,128)S(1)} %get-tuple-element.115) | copy-start | bytes 3145732
